TPU v7x, 512 devices: a whole 4x8x8 slice. The times are simulated.
512 devices in a mesh: date: 64 (over y, z_lo, x), row: 8 (over z_hi, core).
Axes of the slice: x: 4, y: 8, z: 8 (z_hi: 4, z_lo: 2; z = z_hi * 2 + z_lo), core: 2. Of those that a mesh axis runs over, the one named last changes fastest.
Arguments:
- tokens: bfloat16 [128, 128, 16, 384], P('date', 'row'), may hold values from -6 to 6
- clear_flags: int32 [128, 128, 16], P('date', 'row'), may hold values 0 or 1
- date_numbers: int32 [128], P('date'), may hold values from 0 to 1023, as said below
- decay_slopes: float32 [12], replicated, may hold values from 0.00048828125 to 0.03
- time_project: bfloat16 [384, 1152], replicated, may hold values from -0.35 to 0.35
- time_output: bfloat16 [384, 384], replicated, may hold values from -0.3125 to 0.3125
- column_project: bfloat16 [384, 1152], replicated, may hold values from -0.35 to 0.35
- column_output: bfloat16 [384, 384], replicated, may hold values from -0.3125 to 0.3125
- cotangent: bfloat16 [128, 128, 16, 384], P('date', 'row'), may hold values from -6 to 6
Outputs:
- mixed_tokens: bfloat16 [128, 128, 16, 384], P('date', 'row')
- column_project_grad: float32 [384, 1152], P('row', 'date')
- column_output_grad: float32 [384, 384], P('row', 'date')
Inputs may be any that keep to these rules, and one draw needn't show every extreme that they name: `date_numbers`: strictly increasing; consecutive dates lie 1 to 15 days apart.
All inputs are finite; a program needn't handle non-finite values. No bound on the sum of `clear_flags` on one device may be relied on, other than what follows from the above.
Results may differ from a plain program's by a relative error of at most 0.018.
The roundings to bfloat16 on the way count: a program that leaves them out, or rounds other values in their place, can miss the bound.
Values may be sent and summed in bfloat16 or wider, within the bound.
A program may use at most 64 MiB of HBM per device.

v0:
```python
import math

import jax
import jax.numpy as jnp
from jax import lax
from jax.sharding import PartitionSpec as P

epsilon = 1e-06
masked_score = -1e30


def rms_norm(values):
    widened = values.astype(jnp.float32)
    factor = lax.rsqrt(jnp.mean(widened * widened, axis=-1, keepdims=True) + epsilon)
    return (widened * factor).astype(jnp.bfloat16)


def softmax_rows(scores):
    top_score = jnp.max(scores, axis=-1, keepdims=True)
    raised = jnp.exp(scores - top_score)
    return raised / jnp.sum(raised, axis=-1, keepdims=True)


def matmul(left, right):
    return jnp.dot(left, right, preferred_element_type=jnp.float32)


def contract_rows(left, right):
    return lax.dot_general(
        left, right, (((0,), (0,)), ((), ())), preferred_element_type=jnp.float32
    )


def contract_last(left, right):
    return lax.dot_general(
        left, right, (((1,), (1,)), ((), ())), preferred_element_type=jnp.float32
    )


def body(
    tokens,
    clear_flags,
    date_numbers,
    decay_slopes,
    time_project,
    time_output,
    column_project,
    column_output,
    cotangent,
):
    date_local, row_local, column_count, model_width = tokens.shape
    head_count = decay_slopes.shape[0]
    head_size = model_width // head_count
    inverse_root = 1.0 / math.sqrt(head_size)
    patch_count = row_local * column_count
    flat_tokens = tokens.reshape(date_local, patch_count, model_width)
    flags_low = clear_flags.reshape(date_local, patch_count).astype(jnp.bfloat16)
    normed = rms_norm(flat_tokens)
    projected = matmul(normed.reshape(-1, model_width), time_project).astype(jnp.bfloat16)
    projected = projected.reshape(date_local, patch_count, 3 * model_width)
    moved, flags_moved = (
        lax.all_to_all(projected, "date", split_axis=1, concat_axis=0, tiled=True),
        lax.all_to_all(flags_low, "date", split_axis=1, concat_axis=0, tiled=True),
    )
    numbers_all = lax.all_gather(date_numbers, "date", axis=0, tiled=True)
    date_count = moved.shape[0]
    local_patches = moved.shape[1]
    split_heads = moved.reshape(date_count, local_patches, 3, head_count, head_size)
    gap_days = jnp.abs(numbers_all[:, None] - numbers_all[None, :]).astype(jnp.float32)
    time_bias = -decay_slopes[:, None, None] * gap_days[None, :, :]
    positions = jnp.arange(date_count)
    same_date = positions[:, None] == positions[None, :]

    def time_patch(patch_index, buffer):
        series = lax.dynamic_index_in_dim(split_heads, patch_index, 1, keepdims=False)
        day_flags = lax.dynamic_index_in_dim(flags_moved, patch_index, 1, keepdims=False)
        scores = jnp.einsum(
            "qhe,khe->hqk", series[:, 0], series[:, 1], preferred_element_type=jnp.float32
        )
        scores = scores * inverse_root + time_bias
        allowed = (day_flags[None, :] > 0) | same_date
        scores = jnp.where(allowed[None], scores, masked_score)
        weights_low = softmax_rows(scores).astype(jnp.bfloat16)
        patch_heads = jnp.einsum(
            "hqk,khe->qhe", weights_low, series[:, 2], preferred_element_type=jnp.float32
        )
        patch_heads = patch_heads.astype(jnp.bfloat16).reshape(date_count, model_width)
        return lax.dynamic_update_index_in_dim(buffer, patch_heads, patch_index, 1)

    empty_heads = jnp.zeros((date_count, local_patches, model_width), jnp.bfloat16)
    time_heads = lax.fori_loop(0, local_patches, time_patch, empty_heads)
    returned = lax.all_to_all(time_heads, "date", split_axis=0, concat_axis=1, tiled=True)
    update = matmul(returned.reshape(-1, model_width), time_output)
    hidden = (flat_tokens.reshape(-1, model_width).astype(jnp.float32) + update).astype(
        jnp.bfloat16
    )
    hidden = hidden.reshape(date_local, row_local, column_count, model_width)
    plane, plane_grad = (
        lax.all_to_all(hidden, "row", split_axis=2, concat_axis=1, tiled=True),
        lax.all_to_all(cotangent, "row", split_axis=2, concat_axis=1, tiled=True),
    )
    row_count = plane.shape[1]
    local_columns = plane.shape[2]

    def column_date(totals, inputs):
        plane_one, grad_one = inputs
        column_normed = rms_norm(plane_one).reshape(-1, model_width)
        column_qkv = matmul(column_normed, column_project).astype(jnp.bfloat16)
        column_qkv = column_qkv.reshape(row_count, local_columns, 3, head_count, head_size)
        queries = column_qkv[:, :, 0]
        key_block = column_qkv[:, :, 1]
        value_block = column_qkv[:, :, 2]
        column_scores = (
            jnp.einsum("ache,bche->chab", queries, key_block, preferred_element_type=jnp.float32)
            * inverse_root
        )
        weights = softmax_rows(column_scores)
        column_low = weights.astype(jnp.bfloat16)
        column_heads = jnp.einsum(
            "chab,bche->ache", column_low, value_block, preferred_element_type=jnp.float32
        )
        column_heads = column_heads.astype(jnp.bfloat16).reshape(-1, model_width)
        result = plane_one.reshape(-1, model_width).astype(jnp.float32) + matmul(
            column_heads, column_output
        )
        result = result.astype(jnp.bfloat16).reshape(row_count, local_columns, model_width)
        grad_flat = grad_one.reshape(-1, model_width)
        output_term = contract_rows(column_heads, grad_flat)
        heads_grad = contract_last(grad_flat, column_output).astype(jnp.bfloat16)
        heads_grad = heads_grad.reshape(row_count, local_columns, head_count, head_size)
        product_grad = jnp.einsum(
            "ache,bche->chab", heads_grad, value_block, preferred_element_type=jnp.float32
        )
        score_grad = weights * (
            product_grad - jnp.sum(weights * product_grad, axis=-1, keepdims=True)
        )
        score_low = score_grad.astype(jnp.bfloat16)
        query_grad = jnp.einsum(
            "chab,bche->ache", score_low, key_block, preferred_element_type=jnp.float32
        )
        query_grad = (query_grad * inverse_root).astype(jnp.bfloat16)
        key_grad = jnp.einsum(
            "chab,ache->bche", score_low, queries, preferred_element_type=jnp.float32
        )
        key_grad = (key_grad * inverse_root).astype(jnp.bfloat16)
        value_grad = jnp.einsum(
            "chab,ache->bche", column_low, heads_grad, preferred_element_type=jnp.float32
        )
        value_grad = value_grad.astype(jnp.bfloat16)
        qkv_grad = jnp.stack([query_grad, key_grad, value_grad], axis=2).reshape(
            -1, 3 * model_width
        )
        project_term = contract_rows(column_normed, qkv_grad)
        return ((totals[0] + project_term, totals[1] + output_term), result)

    start = (
        jnp.zeros((model_width, 3 * model_width), jnp.float32),
        jnp.zeros((model_width, model_width), jnp.float32),
    )
    totals, result_planes = lax.scan(column_date, start, (plane, plane_grad))
    project_grad, output_grad = totals
    mixed_tokens = lax.all_to_all(result_planes, "row", split_axis=1, concat_axis=2, tiled=True)
    partial_project, partial_output = (
        lax.psum_scatter(
            project_grad.astype(jnp.bfloat16), "row", scatter_dimension=0, tiled=True
        ).astype(jnp.float32),
        lax.psum_scatter(
            output_grad.astype(jnp.bfloat16), "row", scatter_dimension=0, tiled=True
        ).astype(jnp.float32),
    )
    owned_project, owned_output = (
        lax.psum_scatter(partial_project, "date", scatter_dimension=1, tiled=True),
        lax.psum_scatter(partial_output, "date", scatter_dimension=1, tiled=True),
    )
    return (mixed_tokens, owned_project, owned_output)


def solution(mesh):
    return jax.shard_map(
        body,
        mesh=mesh,
        in_specs=(
            P("date", "row", None, None),
            P("date", "row", None),
            P("date"),
            P(),
            P(),
            P(),
            P(),
            P(),
            P("date", "row", None, None),
        ),
        out_specs=(P("date", "row", None, None), P("row", "date"), P("row", "date")),
        check_vma=False,
    )
```

profile of v0, /device:TPU:32, one launch (start us, length us, event | category | flops | bytes accessed | tf_op | source)
XLA Modules:
  0.0 667.4 jit_solution(4211832778568813714)
XLA Ops:
  8.7 12.1 %all-to-all-start.1 = ((bf16[2,64,4]{2,0,1:T(2,128)(2,1)}), bf16[2,64,4]{2,0,1:T(2,128)(2,1)S(1)}, u32[]{:S(2)}, u32[]{:S(2)}) async-start(bf16[2,64,4]{2,0,1:T(2,128)(2,1)} %copy.89), calls=%async_computation.1 | async-start | bytes 65536 | tf_op jit(solution)/shard_map/all_to_all | solution.py:63
  24.1 2.2 copy.87
  26.4 11.2 %all-to-all-start = ((bf16[2,256,1152]{2,0,1:T(2,128)(2,1)}), bf16[2,256,1152]{2,0,1:T(2,128)(2,1)S(1)}, u32[]{:S(2)}, u32[]{:S(2)}) async-start(bf16[2,256,1152]{2,0,1:T(2,128)(2,1)} %copy.87), calls=%async_computation | async-start | bytes 2359296 | tf_op jit(solution)/shard_map/all_to_all | solution.py:62
  39.2 28.7 %all-reduce = s32[128]{0:T(128)S(1)} all-reduce(s32[128]{0:T(128)S(1)} %dynamic-update-slice), channel_id=1, replica_groups=mesh['date'=64,'row'=8] {'date'}, use_global_device_ids=true, to_apply=%add | all-reduce | flops 128 | bytes 1024
  68.6 5.5 reshape.174
  74.2 7.2 %copy.90 = bf16[128,4,3,12,32]{0,4,3,2,1:T(8,128)(2,1)S(1)} copy(bf16[128,4,3,12,32]{4,3,2,1,0:T(8,128)(2,1)} %reshape.174) | data formatting | bytes 2359296
  81.4 14.3 %while.29 = (s32[]{:T(128)}, bf16[128,4,384]{0,2,1:T(8,128)(2,1)S(1)}, bf16[128,4,3,12,32]{0,4,3,2,1:T(8,128)(2,1)S(1)}, bf16[128,4]{0,1:T(4,128)(2,1)S(1)}, f32...) while((s32[]{:T(128)}, bf16[128,4,384]{0,2,1:T(8,128)(2,1)S(1)}, ...), condition=%wide.region_4.5_spmd.clone, body=%wide.region_1.4_spmd.clone.sunk | while | flops 40388736 | bytes 3931737 | solution.py:91
  96.6 13.3 %all-to-all-start.2 = ((bf16[128,4,384]{2,1,0:T(4,128)(2,1)}), bf16[128,4,384]{2,1,0:T(4,128)(2,1)S(1)}, u32[]{:S(2)}, u32[]{:S(2)}) async-start(bf16[128,4,384]{2,1,0:T(4,128)(2,1)} %copy.92), calls=%async_computation.2 | async-start | bytes 786432 | tf_op jit(solution)/shard_map/all_to_all | solution.py:92
  110.8 8.3 %all-to-all-done.2 = bf16[128,4,384]{2,1,0:T(4,128)(2,1)S(1)} async-done(((bf16[128,4,384]{2,1,0:T(4,128)(2,1)}), bf16[128,4,384]{2,1,0:T(4,128)(2,1)S(1)}, u32[]{:S(2)}, u32[]{:S(2)}) %all-to-all-start.2) | async-done | bytes 393248 | tf_op jit(solution)/shard_map/all_to_all | solution.py:92
  119.1 9.4 %all-to-all-start.4 = ((bf16[2,16,16,384]{3,1,0,2:T(8,128)(2,1)}), bf16[2,16,16,384]{3,1,0,2:T(8,128)(2,1)S(1)}, u32[]{:S(2)}, u32[]{:S(2)}) async-start(bf16[2,16,16,384]{3,1,0,2:T(8,128)(2,1)} %copy.96), calls=%async_computation.4 | async-start | bytes 786432 | tf_op jit(solution)/shard_map/all_to_all | solution.py:100
  130.0 13.2 %all-to-all-done.4 = bf16[2,16,16,384]{3,1,0,2:T(8,128)(2,1)S(1)} async-done(((bf16[2,16,16,384]{3,1,0,2:T(8,128)(2,1)}), bf16[2,16,16,384]{3,1,0,2:T(8,128)(2,1)S(1)}, u32[]{:S(2)}, u32[]{:S(2)}) %all-to-all-start.4) | async-done | bytes 393248 | tf_op jit(solution)/shard_map/all_to_all | solution.py:100
  143.3 3.5 all-to-all-start.3
  147.9 14.2 %all-to-all-done.3 = bf16[2,16,16,384]{3,1,0,2:T(8,128)(2,1)S(1)} async-done(((bf16[2,16,16,384]{3,1,0,2:T(8,128)(2,1)}), bf16[2,16,16,384]{3,1,0,2:T(8,128)(2,1)S(1)}, u32[]{:S(2)}, u32[]{:S(2)}) %all-to-all-start.3) | async-done | bytes 393248 | tf_op jit(solution)/shard_map/all_to_all | solution.py:99
  163.2 100.7 %while.30 = (s32[]{:T(128)}, f32[384,1152]{1,0:T(8,128)}, f32[384,384]{1,0:T(8,128)}, bf16[2,128,2,384]{3,2,0,1:T(2,128)(2,1)}, bf16[2,128,2,384]{3,2,1,0:T(2,12...) while((s32[]{:T(128)}, f32[384,1152]{1,0:T(8,128)}, ...), condition=%wide.region_10.11_spmd.clone, body=%wide.region_5.10_spmd.clone.sunk | while | flops 839808384 | bytes 64688072 | solution.py:160
  169.0 3.5 reshape.205
  172.5 3.6 fusion.126
  176.1 2.7 copy.123
  180.3 2.9 fusion.127
  198.7 5.2 copy.126
  203.9 4.1 reshape.206
  213.0 2.0 dynamic-slice_convert_fusion.2
  218.8 3.5 reshape.205
  222.3 3.6 fusion.126
  225.9 2.7 copy.123
  230.1 2.9 fusion.127
  239.1 2.2 convolution_add_fusion.7
  249.6 5.2 copy.126
  254.8 4.1 reshape.206
  268.7 3.5 all-to-all-start.5
  273.5 28.9 %reduce-scatter.9.cloned.1.call-done = bf16[48,384]{1,0:T(8,128)(2,1)} async-done(((bf16[384,384]{1,0:T(8,128)(2,1)}), bf16[48,384]{1,0:T(8,128)(2,1)}) %reduce-scatter.9.cloned.1.call-update) | async-done | bytes 36880
  304.5 42.8 %reduce-scatter.7.cloned.1.call-done = bf16[48,1152]{1,0:T(8,128)(2,1)} async-done(((bf16[384,1152]{1,0:T(8,128)(2,1)}), bf16[48,1152]{1,0:T(8,128)(2,1)}) %reduce-scatter.7.cloned.1.call-update) | async-done | bytes 110608
  348.4 311.0 %all-reduce.5 = (f32[48,1152]{0,1:T(8,128)S(1)}, f32[48,384]{0,1:T(8,128)S(1)}) all-reduce(bf16[48,1152]{0,1:T(8,128)(2,1)S(1)} %copy.108, bf16[48,384]{0,1:T(8,128)(2,1)S(1)} %copy.110), channel_id=3, replica_groups=mesh['date'=64,'row'=8] {'date'}, use_global_device_ids=true, to_apply=%region_12.13.clone | all-reduce | flops 73728 | bytes 442368
  (192 shorter events, 87.3 us)
Async XLA Ops:
  7.2 16.1 %copy-start = (bf16[384,1152]{1,0:T(8,128)(2,1)S(1)}, bf16[384,1152]{1,0:T(8,128)(2,1)}, u32[]{:S(2)}) copy-start(bf16[384,1152]{1,0:T(8,128)(2,1)} %param.17) | copy-start | bytes 2654212
  8.7 17.7 %all-to-all-start.1 = ((bf16[2,64,4]{2,0,1:T(2,128)(2,1)}), bf16[2,64,4]{2,0,1:T(2,128)(2,1)S(1)}, u32[]{:S(2)}, u32[]{:S(2)}) async-start(bf16[2,64,4]{2,0,1:T(2,128)(2,1)} %copy.89), calls=%async_computation.1 | async-start | bytes 65536 | tf_op jit(solution)/shard_map/all_to_all | solution.py:63
  26.3 11.4 %copy-start.19 = (f32[12]{0:T(128)S(1)}, f32[12]{0:T(128)}, u32[]{:S(2)}) copy-start(f32[12]{0:T(128)} %param.16) | copy-start | bytes 148
  26.3 11.4 %copy-start.18 = (u32[512]{0:T(512)S(1)}, u32[512]{0:T(512)}, u32[]{:S(2)}) copy-start(u32[512]{0:T(512)} %constant.104) | copy-start | bytes 6148
  26.3 12.7 %copy-start.20 = (s32[2]{0:T(128)S(1)}, s32[2]{0:T(128)}, u32[]{:S(2)}) copy-start(s32[2]{0:T(128)} %param.15) | copy-start | bytes 28
  26.4 41.7 %all-to-all-start = ((bf16[2,256,1152]{2,0,1:T(2,128)(2,1)}), bf16[2,256,1152]{2,0,1:T(2,128)(2,1)S(1)}, u32[]{:S(2)}, u32[]{:S(2)}) async-start(bf16[2,256,1152]{2,0,1:T(2,128)(2,1)} %copy.87), calls=%async_computation | async-start | bytes 2359296 | tf_op jit(solution)/shard_map/all_to_all | solution.py:62
  74.2 7.2 %copy-start.16 = (bf16[128,4,384]{0,2,1:T(8,128)(2,1)S(1)}, bf16[128,4,384]{0,2,1:T(8,128)(2,1)}, u32[]{:S(2)}) copy-start(bf16[128,4,384]{0,2,1:T(8,128)(2,1)} %custom-call.2) | copy-start | bytes 1179652
  95.6 14.3 %copy-start.15 = (bf16[2,16,16,384]{3,2,1,0:T(8,128)(2,1)S(1)}, bf16[2,16,16,384]{3,2,1,0:T(8,128)(2,1)}, u32[]{:S(2)}) copy-start(bf16[2,16,16,384]{3,2,1,0:T(8,128)(2,1)} %param.21) | copy-start | bytes 1179652
  96.6 22.5 %all-to-all-start.2 = ((bf16[128,4,384]{2,1,0:T(4,128)(2,1)}), bf16[128,4,384]{2,1,0:T(4,128)(2,1)S(1)}, u32[]{:S(2)}, u32[]{:S(2)}) async-start(bf16[128,4,384]{2,1,0:T(4,128)(2,1)} %copy.92), calls=%async_computation.2 | async-start | bytes 786432 | tf_op jit(solution)/shard_map/all_to_all | solution.py:92
  109.9 18.9 %copy-start.14 = (bf16[2,16,16,384]{3,2,1,0:T(8,128)(2,1)S(1)}, bf16[2,16,16,384]{3,2,1,0:T(8,128)(2,1)}, u32[]{:S(2)}) copy-start(bf16[2,16,16,384]{3,2,1,0:T(8,128)(2,1)} %param.13) | copy-start | bytes 1179652
  109.9 18.9 %copy-start.17 = (bf16[384,384]{1,0:T(8,128)(2,1)S(1)}, bf16[384,384]{1,0:T(8,128)(2,1)}, u32[]{:S(2)}) copy-start(bf16[384,384]{1,0:T(8,128)(2,1)} %param.18) | copy-start | bytes 884740
  119.1 24.2 %all-to-all-start.4 = ((bf16[2,16,16,384]{3,1,0,2:T(8,128)(2,1)}), bf16[2,16,16,384]{3,1,0,2:T(8,128)(2,1)S(1)}, u32[]{:S(2)}, u32[]{:S(2)}) async-start(bf16[2,16,16,384]{3,1,0,2:T(8,128)(2,1)} %copy.96), calls=%async_computation.4 | async-start | bytes 786432 | tf_op jit(solution)/shard_map/all_to_all | solution.py:100
  143.3 18.8 %all-to-all-start.3 = ((bf16[2,16,16,384]{3,1,0,2:T(8,128)(2,1)}), bf16[2,16,16,384]{3,1,0,2:T(8,128)(2,1)S(1)}, u32[]{:S(2)}, u32[]{:S(2)}) async-start(bf16[2,16,16,384]{3,1,0,2:T(8,128)(2,1)} %copy.94), calls=%async_computation.3 | async-start | bytes 786432 | tf_op jit(solution)/shard_map/all_to_all | solution.py:99
  146.7 155.7 %reduce-scatter.9.cloned.1.call-start = ((), (), s32[]{:S(2)}) async-start(), calls=%async_computation.9 | async-start | bytes 331776
  184.1 1.8 copy-start.12
  185.9 2.1 copy-start.5
  187.4 1.9 copy-start.9
  188.3 2.1 copy-start.6
  190.4 4.3 copy-start.4
  196.3 1.2 copy-start.7
  203.9 4.1 copy-start.11
  203.9 7.0 %copy-start.1 = (f32[384,1152]{1,0:T(8,128)S(1)}, f32[384,1152]{1,0:T(8,128)}, u32[]{:S(2)}) copy-start(f32[384,1152]{1,0:T(8,128)} %get-tuple-element.399) | copy-start | bytes 5308420 | tf_op jit(solution)/shard_map/while
  233.9 1.8 copy-start.12
  235.7 2.1 copy-start.5
  237.2 1.9 copy-start.9
  238.1 3.2 copy-start.6
  241.3 4.3 copy-start.4
  254.8 4.1 copy-start.11
  254.8 7.0 %copy-start.1 = (f32[384,1152]{1,0:T(8,128)S(1)}, f32[384,1152]{1,0:T(8,128)}, u32[]{:S(2)}) copy-start(f32[384,1152]{1,0:T(8,128)} %get-tuple-element.399) | copy-start | bytes 5308420 | tf_op jit(solution)/shard_map/while
  263.9 2.4 copy-start.3
  266.2 81.0 %reduce-scatter.7.cloned.1.call-start = ((), (), s32[]{:S(2)}) async-start(), calls=%async_computation.8 | async-start | bytes 995328
  268.7 34.6 %all-to-all-start.5 = ((bf16[2,128,2,384]{3,2,0,1:T(2,128)(2,1)}), bf16[2,128,2,384]{3,2,0,1:T(2,128)(2,1)S(1)}, u32[]{:S(2)}, u32[]{:S(2)}) async-start(bf16[2,128,2,384]{3,2,0,1:T(2,128)(2,1)} %get-tuple-element.157), calls=%async_computation.5 | async-start | bytes 786432 | tf_op jit(solution)/shard_map/all_to_all | solution.py:162
  (9 other events, 8.7 us)
Sparse Core Ops, SparseCore 0:
  266.3 36.0 reduce-scatter.8
  305.2 41.9 reduce-scatter.6
where the time goes:
time: 669 us; the launch traced here: 667 us
  blocking collectives  340 us (51%)
  waiting for transfers between devices  108 us (16%)
  local copies, waits for them, and re-layouts  95.1 us (14%)
  starting transfers between devices  53.1 us (8%)
  matrix products  40.3 us (6%)
  between operations  16.3 us (2%)
  other arithmetic  14.6 us (2%)
    unnamed x2, blocking collectives  340 us
    unnamed x4, waiting for transfers between devices  71.7 us
    while x54, local copies, waits for them, and re-layouts  15 us
    unnamed x30, local copies, waits for them, and re-layouts  14.6 us
    all_to_all x1, waiting for transfers between devices, body(): lax.all_to_all(hidden, 'row', split_axis=2, concat_axis=1, tiled=True)  14.2 us
  transfers between devices with their start and end apart: 8, of which 6 were waited for; matrix products, arithmetic and copies ran while one was open for 2% of the time, Pallas kernels for 0%

commit v1 on v0

v1 whole, which is shorter than its diff:
```python
import functools
import math

import jax
import jax.numpy as jnp
from jax import lax
from jax.experimental import pallas as pl
from jax.experimental.pallas import tpu as pltpu
from jax.sharding import PartitionSpec as P

MESH = pl.DeviceIdType.MESH
epsilon = 1e-06
masked_score = -1e30
D = 384
HEADS = 12
GROUPS = 3
inverse_root = 1.0 / math.sqrt(D // HEADS)
bf16, f32 = jnp.bfloat16, jnp.float32


def iota(shape, axis):
    return lax.broadcasted_iota(jnp.int32, shape, axis)


def one_hot(source, width):
    lanes = iota((source.shape[0], width), 1)
    return jnp.where(lanes == source, 1.0, 0.0).astype(bf16)


def matmul(left, right):
    return jnp.dot(left, right, preferred_element_type=f32)


def contract_rows(left, right):
    return lax.dot_general(left, right, (((0,), (0,)), ((), ())), preferred_element_type=f32)


def contract_last(left, right):
    return lax.dot_general(left, right, (((1,), (1,)), ((), ())), preferred_element_type=f32)


def rms_norm(values):
    widened = values.astype(f32)
    factor = lax.rsqrt(jnp.mean(widened * widened, axis=-1, keepdims=True) + epsilon)
    return (widened * factor).astype(bf16)


def head_masks():
    lanes = iota((128, 128), 1) >> 5
    return [lanes == head for head in range(4)]


def stacked(block, masks):
    return jnp.concatenate([jnp.where(mask, block, jnp.zeros_like(block)) for mask in masks], axis=0)


def unstacked(blocks, masks):
    total = jnp.where(masks[0], blocks[0:128], 0.0)
    for head in range(1, 4):
        total = jnp.where(masks[head], blocks[128 * head : 128 * head + 128], total)
    return total


def softmax_block(scores):
    raised = jnp.exp(scores - jnp.max(scores, axis=-1, keepdims=True))
    return raised * (1.0 / jnp.sum(raised, axis=-1, keepdims=True))


def signal(device):
    pl.semaphore_signal(
        pltpu.get_barrier_semaphore(), inc=1, device_id=device, device_id_type=MESH
    )


def remote(source, target, send_sem, recv_sem, device):
    return pltpu.make_async_remote_copy(
        src_ref=source,
        dst_ref=target,
        send_sem=send_sem,
        recv_sem=recv_sem,
        device_id=device,
        device_id_type=MESH,
    )


def wait_bytes(ref, sem):
    pltpu.make_async_copy(ref, ref, sem).wait()


def time_kernel(
    tokens_ref, cotangent_ref, flags_ref, project_ref, output_ref, numbers_ref, slopes_ref,
    rb_ref, rc_ref,
    sa, ra, ss, rs, sc, sb, side, gap_ref, info_ref, base, qkv, heads,
    sem,
):
    d, r = lax.axis_index("date"), lax.axis_index("row")
    parity, octet, kk = d % 2, d // 8, (d // 2) % 4

    def greet_same_row(step, carry):
        signal(((d + step) % 64, r))
        return carry

    def greet_targets(step, carry):
        signal((2 * step + parity, octet))
        signal((8 * r + 2 * (step // 8) + parity, step % 8))
        return carry

    def greet_columns(step, carry):
        signal((d - parity + step // 8, step % 8))
        return carry

    lax.fori_loop(1, 64, greet_same_row, 0)
    lax.fori_loop(0, 32, greet_targets, 0)
    lax.fori_loop(0, 16, greet_columns, 0)

    row = iota((512, 1), 0)
    target = row >> 3
    column = (target & 1) * 8 + (target >> 3)
    source = ((row >> 2) & 1) * 256 + (((target >> 1) & 3) * 4 + (row & 3)) * 16 + column
    sa[...] = matmul(one_hot(source, 512), tokens_ref[...]).astype(bf16).reshape(64, 8, D)
    flipped = contract_rows(
        flags_ref[...].astype(f32).astype(bf16), one_hot(iota((32, 1), 0), 128)
    )
    lane = iota((1, 128), 1)
    first, second = numbers_ref[0], numbers_ref[1]
    extra = jnp.where(lane == 32, first // 32, 0) + jnp.where(lane == 33, second // 32, 0)
    extra = extra + jnp.where(lane == 34, first % 32, 0) + jnp.where(lane == 35, second % 32, 0)
    flipped = flipped + extra.astype(f32)
    for index in range(16):
        ss[index] = flipped[index : index + 1]
    source = ((row >> 4) & 1) * 256 + (row & 15) * 16 + (row >> 5)
    sc[...] = matmul(one_hot(source, 512), cotangent_ref[...]).astype(bf16).reshape(32, 16, D)

    pl.semaphore_wait(pltpu.get_barrier_semaphore(), 63 + 64 + 16)

    def send_tokens(step, carry):
        to = (d + step) % 64
        side_of = (to % 2) * 8 + to // 8
        remote(sa.at[to], ra.at[d], sem.at[0], sem.at[1], (to, r)).start()
        remote(ss.at[side_of], rs.at[d], sem.at[2], sem.at[3], (to, r)).start()
        return carry

    lax.fori_loop(1, 64, send_tokens, 0)
    pltpu.make_async_copy(sa.at[d], ra.at[d], sem.at[1]).start()
    pltpu.make_async_copy(ss.at[parity * 8 + octet], rs.at[d], sem.at[3]).start()
    wait_bytes(rs, sem.at[3])
    wait_bytes(ra, sem.at[1])

    own = parity * 8 + r

    def send_cotangent(step, carry):
        to = (own + step) % 16
        for when in range(2):
            remote(
                sc.at[2 * to + when],
                rc_ref.at[2 * parity + when, pl.ds(pl.multiple_of(16 * r, 16), 16)],
                sem.at[4], sem.at[5], (d - parity + to // 8, to % 8),
            ).start()
        return carry

    lax.fori_loop(1, 16, send_cotangent, 0)
    for when in range(2):
        pltpu.make_async_copy(
            sc.at[2 * own + when],
            rc_ref.at[2 * parity + when, pl.ds(pl.multiple_of(16 * r, 16), 16)],
            sem.at[5],
        ).start()

    for index in range(64):
        side[index : index + 1] = rs[index]
    side_low = side[...].astype(bf16)
    info = jnp.zeros((8, 128), f32)
    pick_row, pick_lane = iota((8, 128), 0), iota((8, 128), 1)
    for when in range(2):
        wanted = jnp.where(pick_row < 4, when * 16 + 4 * kk + pick_row, 32 + when + 2 * (pick_row - 4))
        picked = contract_last(jnp.where(pick_lane == wanted, 1.0, 0.0).astype(bf16), side_low)
        spread = jnp.where(iota((64, 128), 1) == 2 * iota((64, 128), 0) + when, 1.0, 0.0).astype(bf16)
        info = info + matmul(picked.astype(bf16), spread)
    info_ref[...] = info
    days = info[4:5] * 32.0 + info[5:6]
    same_date = iota((128, 128), 0) == iota((128, 128), 1)
    days_down = jnp.sum(jnp.where(same_date, days, 0.0), axis=1, keepdims=True)
    gap_ref[...] = jnp.abs(days_down - days)

    source = ((row & 127) >> 1) * 8 + (row & 1) * 4 + (row >> 7)
    ordered = matmul(one_hot(source, 512), ra[...].reshape(512, D)).astype(bf16)
    base[...] = ordered
    qkv[...] = matmul(rms_norm(ordered), project_ref[...]).astype(bf16)

    def time_patch(patch, carry):
        rows = pl.ds(pl.multiple_of(patch * 128, 128), 128)
        masks = head_masks()
        allowed = (info_ref[pl.ds(patch, 1), :] > 0.5) | (iota((128, 128), 0) == iota((128, 128), 1))
        for group in range(GROUPS):
            queries = qkv[rows, 128 * group : 128 * group + 128]
            keys = stacked(qkv[rows, D + 128 * group : D + 128 * group + 128], masks)
            values = stacked(qkv[rows, 2 * D + 128 * group : 2 * D + 128 * group + 128], masks)
            scores = contract_last(queries, keys)
            weights = []
            for head in range(4):
                block = scores[:, 128 * head : 128 * head + 128] * inverse_root
                block = block + (-slopes_ref[4 * group + head]) * gap_ref[...]
                block = jnp.where(allowed, block, masked_score)
                weights.append(softmax_block(block).astype(bf16))
            heads[rows, 128 * group : 128 * group + 128] = matmul(
                jnp.concatenate(weights, axis=1), values
            ).astype(bf16)
        return carry

    lax.fori_loop(0, 4, time_patch, 0)
    hidden = (base[...].astype(f32) + matmul(heads[...], output_ref[...])).astype(bf16)
    source = ((row >> 2) & 3) * 128 + (row >> 4) * 4 + (row & 3)
    sb[...] = matmul(one_hot(source, 512), hidden).astype(bf16).reshape(32, 16, D)

    slot = 4 * r + kk
    home = r == octet

    def send_hidden(step, carry):
        to = (d // 2 + step) % 32
        remote(sb.at[to], rb_ref.at[slot], sem.at[6], sem.at[7], (2 * to + parity, octet)).start()
        return carry

    lax.fori_loop(1, 32, send_hidden, 0)

    @pl.when(home)
    def _():
        pltpu.make_async_copy(sb.at[d // 2], rb_ref.at[slot], sem.at[7]).start()

    @pl.when(jnp.logical_not(home))
    def _():
        remote(sb.at[d // 2], rb_ref.at[slot], sem.at[6], sem.at[7], (d, octet)).start()

    wait_bytes(rb_ref, sem.at[7])
    wait_bytes(rc_ref, sem.at[5])
    wait_bytes(sa.at[pl.ds(0, 63)], sem.at[0])
    wait_bytes(rs.at[pl.ds(0, 63)], sem.at[2])
    wait_bytes(sc.at[pl.ds(0, 30)], sem.at[4])
    wait_bytes(sb.at[pl.ds(0, 31)], sem.at[6])

    @pl.when(jnp.logical_not(home))
    def _():
        wait_bytes(sb.at[0], sem.at[6])


def column_kernel(
    rb_ref, rc_ref, project_ref, output_ref,
    mixed_ref, project_grad_ref, output_grad_ref,
    plane, normed, qkv, heads_grad, heads, qkv_grad, send_c, recv_c, natural, partial,
    s1, r1, s2, r2, s3, r3, s4, r4,
    sem,
):
    d, r = lax.axis_index("date"), lax.axis_index("row")
    parity, octet = d % 2, d // 8
    x, z_lo, core = d % 4, (d // 4) % 2, r % 2
    own = parity * 8 + r
    partner = (d, r + 1 - 2 * core)

    def greet_rows(step, carry):
        to = (own + step) % 16
        signal((d - parity + to // 8, to % 8))
        return carry

    lax.fori_loop(1, 16, greet_rows, 0)
    signal(partner)
    for step in range(1, 4):
        signal((d - x + (x + step) % 4, r))
    for step in range(1, 8):
        signal(((d + 8 * step) % 64, r))
    for index in range(8):
        signal((d - 4 * z_lo + 4 * core, index))
        signal((d - 4 * z_lo + 4 * (index % 2), index - index % 2 + z_lo))

    row = iota((512, 1), 0)
    source = ((row & 127) >> 2) * 16 + (row & 3) * 4 + (row >> 7)
    hidden = matmul(one_hot(source, 512), rb_ref[...].reshape(512, D)).astype(bf16)
    plane[...] = hidden
    column_normed = rms_norm(hidden)
    normed[...] = column_normed
    qkv[...] = matmul(column_normed, project_ref[...]).astype(bf16)
    heads_grad[...] = contract_last(rc_ref[...].reshape(512, D), output_ref[...]).astype(bf16)

    pl.semaphore_wait(pltpu.get_barrier_semaphore(), 15 + 1 + 3 + 7 + 16)

    def column_date(date, carry):
        rows = pl.ds(pl.multiple_of(date * 128, 128), 128)
        masks = head_masks()
        for group in range(GROUPS):
            lanes = slice(128 * group, 128 * group + 128)
            queries = qkv[rows, 128 * group : 128 * group + 128]
            keys = stacked(qkv[rows, D + 128 * group : D + 128 * group + 128], masks)
            values = stacked(qkv[rows, 2 * D + 128 * group : 2 * D + 128 * group + 128], masks)
            outer = heads_grad[rows, lanes]
            scores = contract_last(queries, keys)
            products = contract_last(outer, values)
            weights_low, scores_low = [], []
            for head in range(4):
                weights = softmax_block(scores[:, 128 * head : 128 * head + 128] * inverse_root)
                product = products[:, 128 * head : 128 * head + 128]
                centre = jnp.sum(weights * product, axis=-1, keepdims=True)
                weights_low.append(weights.astype(bf16))
                scores_low.append((weights * (product - centre)).astype(bf16))
            low = jnp.concatenate(weights_low, axis=1)
            score_low = jnp.concatenate(scores_low, axis=1)
            heads[rows, lanes] = matmul(low, values).astype(bf16)
            qkv_grad[rows, 128 * group : 128 * group + 128] = (
                matmul(score_low, keys) * inverse_root
            ).astype(bf16)
            qkv_grad[rows, D + 128 * group : D + 128 * group + 128] = (
                unstacked(contract_rows(score_low, queries), masks) * inverse_root
            ).astype(bf16)
            qkv_grad[rows, 2 * D + 128 * group : 2 * D + 128 * group + 128] = unstacked(
                contract_rows(low, outer), masks
            ).astype(bf16)
        mixed = plane[rows, :].astype(f32) + matmul(heads[rows, :], output_ref[...])
        send_c[date] = mixed.astype(bf16).reshape(8, 16, D)
        to_date = d - parity + date // 2

        def send_rows(step, inner):
            to = (r + step) % 8
            remote(
                send_c.at[date, to], recv_c.at[date % 2, own], sem.at[0], sem.at[1], (to_date, to)
            ).start()
            return inner

        lax.fori_loop(1, 8, send_rows, 0)

        @pl.when(to_date == d)
        def _():
            pltpu.make_async_copy(send_c.at[date, r], recv_c.at[date % 2, own], sem.at[1]).start()

        @pl.when(to_date != d)
        def _():
            remote(
                send_c.at[date, r], recv_c.at[date % 2, own], sem.at[0], sem.at[1], (to_date, r)
            ).start()

        return carry

    lax.fori_loop(0, 4, column_date, 0)

    natural[0:1152] = contract_rows(qkv_grad[...], normed[...])
    natural[1152:1536] = contract_rows(rc_ref[...].reshape(512, D), heads[...])
    for block in range(64):
        bits = (block % 8) * 8 + (block // 32) * 4 + (block // 8) % 4
        partial[block, 0:18] = natural[18 * bits : 18 * bits + 18]
        partial[block, 18:24] = natural[1152 + 6 * bits : 1152 + 6 * bits + 6]

    for chunk in range(3):
        lanes = slice(128 * chunk, 128 * chunk + 128)
        other = partial[pl.ds(pl.multiple_of(32 - 32 * core, 32), 32), :, lanes]
        s1[chunk] = other.reshape(768, 128).astype(bf16)
        remote(s1.at[chunk], r1.at[chunk], sem.at[2 + chunk], sem.at[5 + chunk], partner).start()
    for chunk in range(3):
        lanes = slice(128 * chunk, 128 * chunk + 128)
        mine = partial[pl.ds(pl.multiple_of(32 * core, 32), 32), :, lanes].reshape(768, 128)
        wait_bytes(r1.at[chunk], sem.at[5 + chunk])
        s2[chunk] = (mine + r1[chunk].astype(f32)).astype(bf16).reshape(4, 192, 128)
        for step in range(1, 4):
            to = (x + step) % 4
            remote(
                s2.at[chunk, to], r2.at[chunk, step - 1], sem.at[8 + chunk], sem.at[11 + chunk],
                (d - x + to, r),
            ).start()
    for chunk in range(3):
        wait_bytes(r2.at[chunk], sem.at[11 + chunk])
        total = s2[chunk, x].astype(f32)
        for step in range(3):
            total = total + r2[chunk, step].astype(f32)
        s3[chunk] = total.reshape(8, 24, 128).astype(bf16)
        for step in range(1, 8):
            to = (octet + step) % 8
            remote(
                s3.at[chunk, to], r3.at[chunk, step - 1], sem.at[14 + chunk], sem.at[17 + chunk],
                ((d + 8 * step) % 64, r),
            ).start()
    for chunk in range(3):
        wait_bytes(r3.at[chunk], sem.at[17 + chunk])
        total = s3[chunk, octet].astype(f32)
        for step in range(7):
            total = total + r3[chunk, step].astype(f32)
        square = jnp.concatenate([total, jnp.zeros((104, 128), f32)], axis=0)
        s4[128 * chunk : 128 * chunk + 128] = jnp.transpose(square).astype(bf16)
    z_slot = (r // 2) * 2 + z_lo
    final_date = d - 4 * z_lo + 4 * core

    def send_final(index, carry):
        to = (r + index) % 8
        remote(
            s4.at[pl.ds(pl.multiple_of(48 * to, 16), 48)], r4.at[z_slot], sem.at[20], sem.at[21],
            (final_date, to),
        ).start()
        return carry

    lax.fori_loop(1, 8, send_final, 0)
    mine_last = s4.at[pl.ds(pl.multiple_of(48 * r, 16), 48)]

    @pl.when(final_date == d)
    def _():
        pltpu.make_async_copy(mine_last, r4.at[z_slot], sem.at[21]).start()

    @pl.when(final_date != d)
    def _():
        remote(mine_last, r4.at[z_slot], sem.at[20], sem.at[21], (final_date, r)).start()

    wait_bytes(recv_c, sem.at[1])
    source = ((row >> 8) * 256) + (row & 15) * 16 + ((row >> 4) & 15)
    mixed_ref[...] = matmul(one_hot(source, 512), recv_c[...].reshape(512, D)).astype(bf16)

    wait_bytes(r4, sem.at[21])
    total = r4[0].astype(f32)
    for index in range(1, 8):
        total = total + r4[index].astype(f32)
    project_grad_ref[...] = total[:, 0:18]
    output_grad_ref[...] = total[:, 18:24]

    wait_bytes(send_c.at[pl.ds(0, 3)], sem.at[0])
    wait_bytes(send_c.at[3, pl.ds(0, 6)], sem.at[0])
    for chunk in range(3):
        wait_bytes(s1.at[chunk], sem.at[2 + chunk])
        wait_bytes(s2.at[chunk, pl.ds(0, 3)], sem.at[8 + chunk])
        wait_bytes(s3.at[chunk, pl.ds(0, 7)], sem.at[14 + chunk])
    wait_bytes(r4.at[pl.ds(0, 7)], sem.at[20])

    @pl.when(final_date != d)
    def _():
        wait_bytes(r4.at[0], sem.at[20])


VM = pl.BlockSpec(memory_space=pltpu.VMEM)
SM = pl.BlockSpec(memory_space=pltpu.SMEM)


def body(
    tokens, clear_flags, date_numbers, decay_slopes, time_project, time_output,
    column_project, column_output, cotangent,
):
    rb, rc = pl.pallas_call(
        time_kernel,
        out_shape=(
            jax.ShapeDtypeStruct((32, 16, D), bf16),
            jax.ShapeDtypeStruct((4, 128, D), bf16),
        ),
        in_specs=[VM] * 5 + [SM] * 2,
        out_specs=(VM, VM),
        scratch_shapes=[
            pltpu.VMEM((64, 8, D), bf16),
            pltpu.VMEM((64, 8, D), bf16),
            pltpu.VMEM((16, 1, 128), f32),
            pltpu.VMEM((64, 1, 128), f32),
            pltpu.VMEM((32, 16, D), bf16),
            pltpu.VMEM((32, 16, D), bf16),
            pltpu.VMEM((64, 128), f32),
            pltpu.VMEM((128, 128), f32),
            pltpu.VMEM((8, 128), f32),
            pltpu.VMEM((512, D), bf16),
            pltpu.VMEM((512, 3 * D), bf16),
            pltpu.VMEM((512, D), bf16),
            pltpu.SemaphoreType.DMA((8,)),
        ],
        compiler_params=pltpu.CompilerParams(
            collective_id=0, has_side_effects=True, vmem_limit_bytes=48 * 1024 * 1024
        ),
        name="time_phase",
    )(
        tokens.reshape(512, D), cotangent.reshape(512, D), clear_flags.reshape(32, 16),
        time_project, time_output, date_numbers, decay_slopes,
    )
    mixed, project_grad, output_grad = pl.pallas_call(
        column_kernel,
        out_shape=(
            jax.ShapeDtypeStruct((512, D), bf16),
            jax.ShapeDtypeStruct((48, 18), f32),
            jax.ShapeDtypeStruct((48, 6), f32),
        ),
        in_specs=[VM] * 4,
        out_specs=(VM, VM, VM),
        scratch_shapes=[
            pltpu.VMEM((512, D), bf16),
            pltpu.VMEM((512, D), bf16),
            pltpu.VMEM((512, 3 * D), bf16),
            pltpu.VMEM((512, D), bf16),
            pltpu.VMEM((512, D), bf16),
            pltpu.VMEM((512, 3 * D), bf16),
            pltpu.VMEM((4, 8, 16, D), bf16),
            pltpu.VMEM((2, 16, 16, D), bf16),
            pltpu.VMEM((1536, D), f32),
            pltpu.VMEM((64, 24, D), f32),
            pltpu.VMEM((3, 768, 128), bf16),
            pltpu.VMEM((3, 768, 128), bf16),
            pltpu.VMEM((3, 4, 192, 128), bf16),
            pltpu.VMEM((3, 3, 192, 128), bf16),
            pltpu.VMEM((3, 8, 24, 128), bf16),
            pltpu.VMEM((3, 7, 24, 128), bf16),
            pltpu.VMEM((D, 128), bf16),
            pltpu.VMEM((8, 48, 128), bf16),
            pltpu.SemaphoreType.DMA((22,)),
        ],
        compiler_params=pltpu.CompilerParams(
            collective_id=1, has_side_effects=True, vmem_limit_bytes=48 * 1024 * 1024
        ),
        name="column_phase",
    )(rb, rc, column_project, column_output)
    return mixed.reshape(tokens.shape), project_grad, output_grad


def solution(mesh):
    return jax.shard_map(
        body,
        mesh=mesh,
        in_specs=(
            P("date", "row", None, None), P("date", "row", None), P("date"),
            P(), P(), P(), P(), P(), P("date", "row", None, None),
        ),
        out_specs=(P("date", "row", None, None), P("row", "date"), P("row", "date")),
        check_vma=False,
    )
```

time: 669 us -> 99.8 us (0.15)
  the two profiles are of different devices: /device:TPU:32 before, /device:TPU:1 now
where the time goes in v1:
time: 99.8 us; the launch traced here: 99.4 us
  Pallas kernels  91.2 us (91%)
  local copies, waits for them, and re-layouts  7.59 us (8%)
    pallas_call x1, Pallas kernels, body(): pl.pallas_call(time_kernel, out_shape=(jax.ShapeDtypeStruct((32, 16, D),...  53.8 us
    pallas_call x1, Pallas kernels, body(): pl.pallas_call(column_kernel, out_shape=(jax.ShapeDtypeStruct((512, D), b...  37.4 us
    unnamed x21, local copies, waits for them, and re-layouts  7.59 us

profile of v1, /device:TPU:1, one launch (start us, length us, event | category | flops | bytes accessed | tf_op | source)
XLA Modules:
  0.0 99.4 jit_solution(7337564390968703856)
XLA Ops:
  0.6 0.0 copy-start.7
  0.6 0.0 copy-start.8
  0.7 0.6 copy-done.7
  1.3 0.0 copy-done.8
  1.3 0.0 copy-start
  1.3 1.2 %copy-done = bf16[384,1152]{1,0:T(8,128)(2,1)S(1)} copy-done((bf16[384,1152]{1,0:T(8,128)(2,1)S(1)}, bf16[384,1152]{1,0:T(8,128)(2,1)}, u32[]{:S(2)}) %copy-start) | copy-done | bytes 884760
  2.5 0.0 copy-start.2
  2.5 1.0 copy-done.2
  3.5 0.0 copy-start.3
  3.5 1.0 copy-done.3
  4.5 0.0 copy-start.4
  4.5 1.0 copy-done.4
  5.4 0.0 copy-start.6
  5.4 0.7 copy-done.6
  6.1 0.0 copy-start.1
  6.1 0.0 copy-start.5
  6.2 53.8 %time_phase.1 = (bf16[32,16,384]{2,1,0:T(8,128)(2,1)S(1)}, bf16[4,128,384]{2,1,0:T(8,128)(2,1)S(1)}) custom-call(bf16[512,384]{1,0:T(8,128)(2,1)S(1)} %bitcast.4, bf16[512,384]{1,0:T(8,128)(2,1)S(1)} %bitcast.5, s32[32,16]{1,0:T(8,128)S(1)} %bitcast.7, bf16[384,1152]{1,0:T(8,128)(2,1)S(1)} %copy-done, bf16[384,384]{1,0:T(8,128)(2,1)S(1)} %copy-done.4, ...), custom_call_target="tpu_custom_call" | custom-call | tf_op jit(solution)/shard_map/time_phase/pallas_call | solution.py:437
  60.0 0.0 copy-done.1
  60.0 0.0 copy-done.5
  60.0 37.4 %column_phase.1 = (bf16[512,384]{1,0:T(8,128)(2,1)S(1)}, f32[48,18]{1,0:T(8,128)S(1)}, f32[48,6]{1,0:T(8,128)S(1)}) custom-call(bf16[32,16,384]{2,1,0:T(8,128)(2,1)S(1)} %get-tuple-element.8.rb_ref, bf16[4,128,384]{2,1,0:T(8,128)(2,1)S(1)} %get-tuple-element.9.rc_ref, bf16[384,1152]{1,0:T(8,128)(2,1)S(1)} %copy-done.1, bf16[384,384]{1,0:T(8,128)(2,1)S(1)} %copy-done.5), custom_call_target="tpu_custom_call" | custom-call | tf_op jit(solution)/shard_map/column_phase/pallas_call | solution.py:468
  97.3 0.7 copy.13
  98.0 0.7 copy.12
  98.7 0.7 copy.15
Async XLA Ops:
  0.6 0.7 copy-start.7
  0.6 0.7 copy-start.8
  1.3 1.2 %copy-start = (bf16[384,1152]{1,0:T(8,128)(2,1)S(1)}, bf16[384,1152]{1,0:T(8,128)(2,1)}, u32[]{:S(2)}) copy-start(bf16[384,1152]{1,0:T(8,128)(2,1)} %project_ref.2) | copy-start | bytes 2654212
  2.5 1.0 %copy-start.2 = (bf16[2,16,16,384]{3,2,1,0:T(8,128)(2,1)S(1)}, bf16[2,16,16,384]{3,2,1,0:T(8,128)(2,1)}, u32[]{:S(2)}) copy-start(bf16[2,16,16,384]{3,2,1,0:T(8,128)(2,1)} %param.9) | copy-start | bytes 1179652
  3.5 1.0 %copy-start.3 = (bf16[2,16,16,384]{3,2,1,0:T(8,128)(2,1)S(1)}, bf16[2,16,16,384]{3,2,1,0:T(8,128)(2,1)}, u32[]{:S(2)}) copy-start(bf16[2,16,16,384]{3,2,1,0:T(8,128)(2,1)} %param.17) | copy-start | bytes 1179652
  4.5 1.0 copy-start.4
  5.4 0.7 copy-start.6
  6.1 53.8 %copy-start.1 = (bf16[384,1152]{1,0:T(8,128)(2,1)S(1)}, bf16[384,1152]{1,0:T(8,128)(2,1)}, u32[]{:S(2)}) copy-start(bf16[384,1152]{1,0:T(8,128)(2,1)} %project_ref.3) | copy-start | bytes 2654212
  6.1 53.8 %copy-start.5 = (bf16[384,384]{1,0:T(8,128)(2,1)S(1)}, bf16[384,384]{1,0:T(8,128)(2,1)}, u32[]{:S(2)}) copy-start(bf16[384,384]{1,0:T(8,128)(2,1)} %output_ref.3) | copy-start | bytes 884740

commit v2 on v1

v2 whole, which is shorter than its diff:
```python
import functools
import math

import jax
import jax.numpy as jnp
from jax import lax
from jax.experimental import pallas as pl
from jax.experimental.pallas import tpu as pltpu
from jax.sharding import PartitionSpec as P

MESH = pl.DeviceIdType.MESH
epsilon = 1e-06
masked_score = -1e30
D = 384
HEADS = 12
GROUPS = 3
inverse_root = 1.0 / math.sqrt(D // HEADS)
bf16, f32 = jnp.bfloat16, jnp.float32


def iota(shape, axis):
    return lax.broadcasted_iota(jnp.int32, shape, axis)


def one_hot(source, width):
    lanes = iota((source.shape[0], width), 1)
    return jnp.where(lanes == source, 1.0, 0.0).astype(bf16)


def matmul(left, right):
    return jnp.dot(left, right, preferred_element_type=f32)


def contract_rows(left, right):
    return lax.dot_general(left, right, (((0,), (0,)), ((), ())), preferred_element_type=f32)


def contract_last(left, right):
    return lax.dot_general(left, right, (((1,), (1,)), ((), ())), preferred_element_type=f32)


def rms_norm(values):
    widened = values.astype(f32)
    factor = lax.rsqrt(jnp.mean(widened * widened, axis=-1, keepdims=True) + epsilon)
    return (widened * factor).astype(bf16)


def head_masks():
    lanes = iota((128, 128), 1) >> 5
    return [lanes == head for head in range(4)]


def stacked(block, masks):
    return jnp.concatenate([jnp.where(mask, block, jnp.zeros_like(block)) for mask in masks], axis=0)


def unstacked(blocks, masks):
    total = jnp.where(masks[0], blocks[0:128], 0.0)
    for head in range(1, 4):
        total = jnp.where(masks[head], blocks[128 * head : 128 * head + 128], total)
    return total


def softmax_block(scores):
    raised = jnp.exp(scores - jnp.max(scores, axis=-1, keepdims=True))
    return raised * (1.0 / jnp.sum(raised, axis=-1, keepdims=True))


def signal(device):
    pl.semaphore_signal(
        pltpu.get_barrier_semaphore(), inc=1, device_id=device, device_id_type=MESH
    )


def remote(source, target, send_sem, recv_sem, device):
    return pltpu.make_async_remote_copy(
        src_ref=source,
        dst_ref=target,
        send_sem=send_sem,
        recv_sem=recv_sem,
        device_id=device,
        device_id_type=MESH,
    )


def wait_bytes(ref, sem):
    pltpu.make_async_copy(ref, ref, sem).wait()


def swing(step, count):
    half = (step + 1) // 2
    return jnp.where(step % 2 == 1, half, count - half)


def layer_kernel(
    tokens_hbm, cotangent_hbm, flags_hbm, time_project_hbm, time_output_hbm,
    column_project_hbm, column_output_hbm, numbers_hbm, slopes_hbm,
    recv_c, r4,
    tokens_ref, rc_in, flags_ref, project_ref, output_ref, column_project_ref, column_output_ref,
    numbers_ref, slopes_ref,
    sa, ra, ss, rs, sc, sb, rb_ref, rc_ref, side, gap_ref, info_ref, base, qkv, heads,
    plane, normed, heads_grad, qkv_grad, send_c, natural, partial_x, partial_y,
    s1, r1, s2x, r2x, s3x, r3x, s2y, r2y, s3y, r3y, s4,
    sem, grad_sem, load_sem,
):
    d, r = lax.axis_index("date"), lax.axis_index("row")
    parity, octet, kk = d % 2, d // 8, (d // 2) % 4
    x, z_lo, core = d % 4, (d // 4) % 2, r % 2
    own = parity * 8 + r
    partner = (d, r + 1 - 2 * core)

    loads = [
        pltpu.make_async_copy(source, target, load_sem.at[index])
        for index, (source, target) in enumerate((
            (tokens_hbm, tokens_ref), (flags_hbm, flags_ref), (numbers_hbm, numbers_ref),
            (cotangent_hbm, rc_in), (time_project_hbm, project_ref), (slopes_hbm, slopes_ref),
            (time_output_hbm, output_ref), (column_output_hbm, column_output_ref),
            (column_project_hbm, column_project_ref),
        ))
    ]
    for load in loads:
        load.start()

    def greet_same_row(step, carry):
        signal(((d + step) % 64, r))
        return carry

    def greet_targets(step, carry):
        signal((2 * step + parity, octet))
        signal((8 * r + 2 * (step // 8) + parity, step % 8))
        return carry

    def greet_columns(step, carry):
        to = (own + step) % 16
        signal((d - parity + to // 8, to % 8))
        return carry

    lax.fori_loop(1, 64, greet_same_row, 0)
    lax.fori_loop(0, 32, greet_targets, 0)
    lax.fori_loop(1, 16, greet_columns, 0)
    signal(partner)
    for index in range(8):
        signal((d - 4 * z_lo + 4 * core, index))
        signal((d - 4 * z_lo + 4 * (index % 2), index - index % 2 + z_lo))

    row = iota((512, 1), 0)
    loads[0].wait()
    target = row >> 3
    column = (target & 1) * 8 + (target >> 3)
    source = ((row >> 2) & 1) * 256 + (((target >> 1) & 3) * 4 + (row & 3)) * 16 + column
    sa[...] = matmul(one_hot(source, 512), tokens_ref[...]).astype(bf16).reshape(64, 8, D)
    loads[1].wait()
    flipped = contract_rows(
        flags_ref[...].astype(f32).astype(bf16), one_hot(iota((32, 1), 0), 128)
    )
    loads[2].wait()
    lane = iota((1, 128), 1)
    first, second = numbers_ref[0], numbers_ref[1]
    extra = jnp.where(lane == 32, first // 32, 0) + jnp.where(lane == 33, second // 32, 0)
    extra = extra + jnp.where(lane == 34, first % 32, 0) + jnp.where(lane == 35, second % 32, 0)
    flipped = flipped + extra.astype(f32)
    for index in range(16):
        ss[index] = flipped[index : index + 1]

    pl.semaphore_wait(pltpu.get_barrier_semaphore(), 63 + 64 + 15 + 1 + 16)

    def send_tokens(step, carry):
        to = (d + swing(step, 64)) % 64
        remote(sa.at[to], ra.at[d], sem.at[0], sem.at[1], (to, r)).start()
        return carry

    def send_side(step, carry):
        to = (d + swing(step, 64)) % 64
        side_of = (to % 2) * 8 + to // 8
        remote(ss.at[side_of], rs.at[d], sem.at[2], sem.at[3], (to, r)).start()
        return carry

    def send_cotangent(step, carry):
        to = (own + step) % 16
        for when in range(2):
            remote(
                sc.at[2 * to + when],
                rc_ref.at[2 * parity + when, pl.ds(pl.multiple_of(16 * r, 16), 16)],
                sem.at[4], sem.at[5], (d - parity + to // 8, to % 8),
            ).start()
        return carry

    lax.fori_loop(1, 64, send_tokens, 0)
    pltpu.make_async_copy(sa.at[d], ra.at[d], sem.at[1]).start()
    lax.fori_loop(1, 64, send_side, 0)
    pltpu.make_async_copy(ss.at[parity * 8 + octet], rs.at[d], sem.at[3]).start()
    loads[3].wait()
    source = ((row >> 4) & 1) * 256 + (row & 15) * 16 + (row >> 5)
    sc[...] = matmul(one_hot(source, 512), rc_in[...]).astype(bf16).reshape(32, 16, D)
    lax.fori_loop(1, 16, send_cotangent, 0)
    for when in range(2):
        pltpu.make_async_copy(
            sc.at[2 * own + when],
            rc_ref.at[2 * parity + when, pl.ds(pl.multiple_of(16 * r, 16), 16)],
            sem.at[5],
        ).start()
    for load in loads[4:]:
        load.wait()

    wait_bytes(ra, sem.at[1])
    source = ((row & 127) >> 1) * 8 + (row & 1) * 4 + (row >> 7)
    ordered = matmul(one_hot(source, 512), ra[...].reshape(512, D)).astype(bf16)
    base[...] = ordered
    qkv[...] = matmul(rms_norm(ordered), project_ref[...]).astype(bf16)

    wait_bytes(rs, sem.at[3])
    for index in range(64):
        side[index : index + 1] = rs[index]
    side_low = side[...].astype(bf16)
    info = jnp.zeros((8, 128), f32)
    pick_row, pick_lane = iota((8, 128), 0), iota((8, 128), 1)
    for when in range(2):
        wanted = jnp.where(pick_row < 4, when * 16 + 4 * kk + pick_row, 32 + when + 2 * (pick_row - 4))
        picked = contract_last(jnp.where(pick_lane == wanted, 1.0, 0.0).astype(bf16), side_low)
        spread = jnp.where(iota((64, 128), 1) == 2 * iota((64, 128), 0) + when, 1.0, 0.0).astype(bf16)
        info = info + matmul(picked.astype(bf16), spread)
    info_ref[...] = info
    days = info[4:5] * 32.0 + info[5:6]
    same_date = iota((128, 128), 0) == iota((128, 128), 1)
    days_down = jnp.sum(jnp.where(same_date, days, 0.0), axis=1, keepdims=True)
    gap_ref[...] = jnp.abs(days_down - days)

    def time_patch(patch, carry):
        rows = pl.ds(pl.multiple_of(patch * 128, 128), 128)
        masks = head_masks()
        allowed = (info_ref[pl.ds(patch, 1), :] > 0.5) | (iota((128, 128), 0) == iota((128, 128), 1))
        for group in range(GROUPS):
            queries = qkv[rows, 128 * group : 128 * group + 128]
            keys = stacked(qkv[rows, D + 128 * group : D + 128 * group + 128], masks)
            values = stacked(qkv[rows, 2 * D + 128 * group : 2 * D + 128 * group + 128], masks)
            scores = contract_last(queries, keys)
            weights = []
            for head in range(4):
                block = scores[:, 128 * head : 128 * head + 128] * inverse_root
                block = block + (-slopes_ref[4 * group + head]) * gap_ref[...]
                block = jnp.where(allowed, block, masked_score)
                weights.append(softmax_block(block).astype(bf16))
            heads[rows, 128 * group : 128 * group + 128] = matmul(
                jnp.concatenate(weights, axis=1), values
            ).astype(bf16)
        return carry

    slot = 2 * (4 * r + kk)
    home = r == octet

    def time_half(half, carry):
        lax.fori_loop(2 * half, 2 * half + 2, time_patch, 0)
        rows = pl.ds(pl.multiple_of(half * 256, 256), 256)
        hidden = (base[rows, :].astype(f32) + matmul(heads[rows, :], output_ref[...])).astype(bf16)
        small = iota((256, 1), 0)
        source = ((small >> 2) & 1) * 128 + (small >> 3) * 4 + (small & 3)
        sb[half] = matmul(one_hot(source, 256), hidden).astype(bf16).reshape(32, 8, D)

        def send_hidden(step, inner):
            to = (d // 2 + swing(step, 32)) % 32
            remote(
                sb.at[half, to], rb_ref.at[slot + half], sem.at[6], sem.at[7],
                (2 * to + parity, octet),
            ).start()
            return inner

        lax.fori_loop(1, 32, send_hidden, 0)

        @pl.when(home)
        def _():
            pltpu.make_async_copy(sb.at[half, d // 2], rb_ref.at[slot + half], sem.at[7]).start()

        @pl.when(jnp.logical_not(home))
        def _():
            remote(
                sb.at[half, d // 2], rb_ref.at[slot + half], sem.at[6], sem.at[7], (d, octet)
            ).start()

        return carry

    lax.fori_loop(0, 2, time_half, 0)

    wait_bytes(rc_ref, sem.at[5])
    heads_grad[...] = contract_last(rc_ref[...].reshape(512, D), column_output_ref[...]).astype(bf16)
    wait_bytes(rb_ref, sem.at[7])

    source = ((row & 127) >> 2) * 16 + (row & 3) * 4 + (row >> 7)
    hidden = matmul(one_hot(source, 512), rb_ref[...].reshape(512, D)).astype(bf16)
    plane[...] = hidden
    column_normed = rms_norm(hidden)
    normed[...] = column_normed
    qkv[...] = matmul(column_normed, column_project_ref[...]).astype(bf16)

    def column_date(date, carry):
        rows = pl.ds(pl.multiple_of(date * 128, 128), 128)
        masks = head_masks()
        for group in range(GROUPS):
            lanes = slice(128 * group, 128 * group + 128)
            queries = qkv[rows, 128 * group : 128 * group + 128]
            keys = stacked(qkv[rows, D + 128 * group : D + 128 * group + 128], masks)
            values = stacked(qkv[rows, 2 * D + 128 * group : 2 * D + 128 * group + 128], masks)
            outer = heads_grad[rows, lanes]
            scores = contract_last(queries, keys)
            products = contract_last(outer, values)
            weights_low, scores_low = [], []
            for head in range(4):
                weights = softmax_block(scores[:, 128 * head : 128 * head + 128] * inverse_root)
                product = products[:, 128 * head : 128 * head + 128]
                centre = jnp.sum(weights * product, axis=-1, keepdims=True)
                weights_low.append(weights.astype(bf16))
                scores_low.append((weights * (product - centre)).astype(bf16))
            low = jnp.concatenate(weights_low, axis=1)
            score_low = jnp.concatenate(scores_low, axis=1)
            heads[rows, lanes] = matmul(low, values).astype(bf16)
            qkv_grad[rows, 128 * group : 128 * group + 128] = (
                matmul(score_low, keys) * inverse_root
            ).astype(bf16)
            qkv_grad[rows, D + 128 * group : D + 128 * group + 128] = (
                unstacked(contract_rows(score_low, queries), masks) * inverse_root
            ).astype(bf16)
            qkv_grad[rows, 2 * D + 128 * group : 2 * D + 128 * group + 128] = unstacked(
                contract_rows(low, outer), masks
            ).astype(bf16)
        mixed = plane[rows, :].astype(f32) + matmul(heads[rows, :], column_output_ref[...])
        send_c[date] = mixed.astype(bf16).reshape(8, 16, D)
        to_date = d - parity + date // 2

        def send_rows(step, inner):
            to = (r + swing(step, 8)) % 8
            remote(
                send_c.at[date, to], recv_c.at[date % 2, own], sem.at[8], sem.at[9], (to_date, to)
            ).start()
            return inner

        lax.fori_loop(1, 8, send_rows, 0)

        @pl.when(to_date == d)
        def _():
            pltpu.make_async_copy(send_c.at[date, r], recv_c.at[date % 2, own], sem.at[9]).start()

        @pl.when(to_date != d)
        def _():
            remote(
                send_c.at[date, r], recv_c.at[date % 2, own], sem.at[8], sem.at[9], (to_date, r)
            ).start()

        return carry

    lax.fori_loop(0, 4, column_date, 0)

    natural[0:1152] = contract_rows(qkv_grad[...], normed[...])
    natural[1152:1536] = contract_rows(rc_ref[...].reshape(512, D), heads[...])
    for block in range(64):
        bits = (block % 8) * 8 + (block // 32) * 4 + (block // 8) % 4
        flipped_block = (block // 32) * 32 + (block % 8) * 4 + (block // 8) % 4
        partial_y[flipped_block, 0:18] = natural[18 * bits : 18 * bits + 18, 256:384]
        partial_y[flipped_block, 18:24] = natural[1152 + 6 * bits : 1152 + 6 * bits + 6, 256:384]
        partial_x[block, 0:18] = natural[18 * bits : 18 * bits + 18, 0:256]
        partial_x[block, 18:24] = natural[1152 + 6 * bits : 1152 + 6 * bits + 6, 0:256]

    along_x = (x, 4, 1, (1, 3, 2), lambda step: (d - x + (x + step) % 4, r))
    along_y = (octet, 8, 8, (1, 7, 2, 6, 3, 5, 4), lambda step: ((d + 8 * step) % 64, r))
    plans = (
        (2, partial_y, 0, along_y, s2y, r2y, along_x, s3y, r3y),
        (0, partial_x, 0, along_x, s2x.at[0], r2x.at[0], along_y, s3x.at[0], r3x.at[0]),
        (1, partial_x, 128, along_x, s2x.at[1], r2x.at[1], along_y, s3x.at[1], r3x.at[1]),
    )

    def exchange(axis, sent, received, send_sem, recv_sem):
        me, size, _, steps, device = axis
        for step in steps:
            remote(
                sent.at[(me + step) % size], received.at[step - 1], send_sem, recv_sem, device(step)
            ).start()

    def gathered(axis, sent, received, recv_sem):
        me, size = axis[:2]
        wait_bytes(received, recv_sem)
        total = sent[me].astype(f32)
        for index in range(size - 1):
            total = total + received[index].astype(f32)
        return total

    for chunk, partial, low, *_ in plans:
        other = partial[pl.ds(pl.multiple_of(32 - 32 * core, 32), 32), :, low : low + 128]
        s1[chunk] = other.reshape(768, 128).astype(bf16)
        remote(
            s1.at[chunk], r1.at[chunk], grad_sem.at[chunk], grad_sem.at[3 + chunk], partner
        ).start()
    for chunk, partial, low, first_axis, sent, received, *_ in plans:
        mine = partial[pl.ds(pl.multiple_of(32 * core, 32), 32), :, low : low + 128].reshape(768, 128)
        wait_bytes(r1.at[chunk], grad_sem.at[3 + chunk])
        size = first_axis[1]
        sent[...] = (mine + r1[chunk].astype(f32)).astype(bf16).reshape(size, 768 // size, 128)
        exchange(first_axis, sent, received, grad_sem.at[6 + chunk], grad_sem.at[9 + chunk])
    for chunk, _, _, first_axis, sent, received, second_axis, sent_next, received_next in plans:
        total = gathered(first_axis, sent, received, grad_sem.at[9 + chunk])
        sent_next[...] = total.reshape(second_axis[1], 24, 128).astype(bf16)
        exchange(
            second_axis, sent_next, received_next, grad_sem.at[12 + chunk], grad_sem.at[15 + chunk]
        )
    for chunk, _, _, _, _, _, second_axis, sent_next, received_next in plans:
        total = gathered(second_axis, sent_next, received_next, grad_sem.at[15 + chunk])
        square = jnp.concatenate([total, jnp.zeros((104, 128), f32)], axis=0)
        s4[128 * chunk : 128 * chunk + 128] = jnp.transpose(square).astype(bf16)
    z_slot = (r // 2) * 2 + z_lo
    final_date = d - 4 * z_lo + 4 * core

    def send_final(step, carry):
        to = (r + swing(step, 8)) % 8
        remote(
            s4.at[pl.ds(pl.multiple_of(48 * to, 16), 48)], r4.at[z_slot],
            grad_sem.at[18], grad_sem.at[19], (final_date, to),
        ).start()
        return carry

    lax.fori_loop(1, 8, send_final, 0)
    mine_last = s4.at[pl.ds(pl.multiple_of(48 * r, 16), 48)]

    @pl.when(final_date == d)
    def _():
        pltpu.make_async_copy(mine_last, r4.at[z_slot], grad_sem.at[19]).start()

    @pl.when(final_date != d)
    def _():
        remote(
            mine_last, r4.at[z_slot], grad_sem.at[18], grad_sem.at[19], (final_date, r)
        ).start()

    wait_bytes(sa.at[pl.ds(0, 63)], sem.at[0])
    wait_bytes(rs.at[pl.ds(0, 63)], sem.at[2])
    wait_bytes(sc.at[pl.ds(0, 30)], sem.at[4])
    wait_bytes(sb.at[0], sem.at[6])
    wait_bytes(sb.at[1, pl.ds(0, 30)], sem.at[6])

    @pl.when(jnp.logical_not(home))
    def _():
        wait_bytes(sb.at[0, pl.ds(0, 2)], sem.at[6])

    wait_bytes(send_c.at[pl.ds(0, 3)], sem.at[8])
    wait_bytes(send_c.at[3, pl.ds(0, 6)], sem.at[8])
    for chunk, _, _, first_axis, sent, received, second_axis, sent_next, received_next in plans:
        wait_bytes(s1.at[chunk], grad_sem.at[chunk])
        wait_bytes(received, grad_sem.at[6 + chunk])
        wait_bytes(received_next, grad_sem.at[12 + chunk])
    wait_bytes(recv_c, sem.at[9])
    wait_bytes(r4, grad_sem.at[19])
    wait_bytes(r4.at[pl.ds(0, 7)], grad_sem.at[18])

    @pl.when(final_date != d)
    def _():
        wait_bytes(r4.at[0], grad_sem.at[18])


def finish_kernel(recv_c, r4, mixed_ref, project_grad_ref, output_grad_ref):
    small = iota((256, 1), 0)
    order = one_hot((small & 15) * 16 + (small >> 4), 256)
    for when in range(2):
        mixed_ref[256 * when : 256 * when + 256] = matmul(
            order, recv_c[when].reshape(256, D)
        ).astype(bf16)
    total = r4[0].astype(f32)
    for index in range(1, 8):
        total = total + r4[index].astype(f32)
    project_grad_ref[...] = total[:, 0:18]
    output_grad_ref[...] = total[:, 18:24]


VM = pl.BlockSpec(memory_space=pltpu.VMEM)
HB = pl.BlockSpec(memory_space=pltpu.HBM)


def body(
    tokens, clear_flags, date_numbers, decay_slopes, time_project, time_output,
    column_project, column_output, cotangent,
):
    vmem = pltpu.VMEM
    recv_c, r4 = pl.pallas_call(
        layer_kernel,
        out_shape=(
            jax.ShapeDtypeStruct((2, 16, 16, D), bf16),
            jax.ShapeDtypeStruct((8, 48, 128), bf16),
        ),
        in_specs=[HB] * 9,
        out_specs=(VM, VM),
        scratch_shapes=[
            vmem((512, D), bf16),
            vmem((512, D), bf16),
            vmem((32, 16), jnp.int32),
            vmem((D, 3 * D), bf16),
            vmem((D, D), bf16),
            vmem((D, 3 * D), bf16),
            vmem((D, D), bf16),
            pltpu.SMEM((2,), jnp.int32),
            pltpu.SMEM((HEADS,), f32),
            vmem((64, 8, D), bf16),
            vmem((64, 8, D), bf16),
            vmem((16, 1, 128), f32),
            vmem((64, 1, 128), f32),
            vmem((32, 16, D), bf16),
            vmem((2, 32, 8, D), bf16),
            vmem((64, 8, D), bf16),
            vmem((4, 128, D), bf16),
            vmem((64, 128), f32),
            vmem((128, 128), f32),
            vmem((8, 128), f32),
            vmem((512, D), bf16),
            vmem((512, 3 * D), bf16),
            vmem((512, D), bf16),
            vmem((512, D), bf16),
            vmem((512, D), bf16),
            vmem((512, D), bf16),
            vmem((512, 3 * D), bf16),
            vmem((4, 8, 16, D), bf16),
            vmem((1536, D), f32),
            vmem((64, 24, 256), f32),
            vmem((64, 24, 128), f32),
            vmem((3, 768, 128), bf16),
            vmem((3, 768, 128), bf16),
            vmem((2, 4, 192, 128), bf16),
            vmem((2, 3, 192, 128), bf16),
            vmem((2, 8, 24, 128), bf16),
            vmem((2, 7, 24, 128), bf16),
            vmem((8, 96, 128), bf16),
            vmem((7, 96, 128), bf16),
            vmem((4, 24, 128), bf16),
            vmem((3, 24, 128), bf16),
            vmem((D, 128), bf16),
            pltpu.SemaphoreType.DMA((10,)),
            pltpu.SemaphoreType.DMA((20,)),
            pltpu.SemaphoreType.DMA((9,)),
        ],
        compiler_params=pltpu.CompilerParams(
            collective_id=0, has_side_effects=True, vmem_limit_bytes=48 * 1024 * 1024
        ),
        name="layer",
    )(
        tokens.reshape(512, D), cotangent.reshape(512, D), clear_flags.reshape(32, 16),
        time_project, time_output, column_project, column_output, date_numbers, decay_slopes,
    )
    mixed, project_grad, output_grad = pl.pallas_call(
        finish_kernel,
        out_shape=(
            jax.ShapeDtypeStruct((512, D), bf16),
            jax.ShapeDtypeStruct((48, 18), f32),
            jax.ShapeDtypeStruct((48, 6), f32),
        ),
        in_specs=[VM] * 2,
        out_specs=(VM, VM, VM),
        name="finish",
    )(recv_c, r4)
    return mixed.reshape(tokens.shape), project_grad, output_grad


def solution(mesh):
    return jax.shard_map(
        body,
        mesh=mesh,
        in_specs=(
            P("date", "row", None, None), P("date", "row", None), P("date"),
            P(), P(), P(), P(), P(), P("date", "row", None, None),
        ),
        out_specs=(P("date", "row", None, None), P("row", "date"), P("row", "date")),
        check_vma=False,
    )
```

time: 99.8 us -> 97.7 us (0.979)
  Pallas kernels: 91.2 us -> 85.4 us
  local copies, waits for them, and re-layouts: 7.59 us -> 11.1 us
    pallas_call x2, Pallas kernels: 91.2 us -> 85.4 us  [the longest x1 83.4 us: body(): pl.pallas_call(layer_kernel, out_shape=(jax.ShapeDtypeStruct((2, 16, 16,...]
    unnamed x21 -> x26, local copies, waits for them, and re-layouts: 7.59 us -> 11.1 us
where the time goes in v2:
time: 97.7 us; the launch traced here: 97.2 us
  Pallas kernels  85.4 us (87%)
  local copies, waits for them, and re-layouts  11.1 us (11%)
    pallas_call x1, Pallas kernels, body(): pl.pallas_call(layer_kernel, out_shape=(jax.ShapeDtypeStruct((2, 16, 16,...  83.4 us
    unnamed x26, local copies, waits for them, and re-layouts  11.1 us
    pallas_call x1, Pallas kernels, body(): pl.pallas_call(finish_kernel, out_shape=(jax.ShapeDtypeStruct((512, D), b...  2.05 us

profile of v2, /device:TPU:1, one launch (start us, length us, event | category | flops | bytes accessed | tf_op | source)
XLA Modules:
  0.0 97.2 jit_solution(7054319061662960713)
XLA Ops:
  0.6 0.0 copy-start.9
  0.6 0.0 copy-start.10
  0.7 0.6 copy-done.9
  1.3 0.0 copy-done.10
  1.3 0.0 copy-start
  1.3 1.2 %copy-done = bf16[384,1152]{1,0:T(8,128)(2,1)S(1)} copy-done((bf16[384,1152]{1,0:T(8,128)(2,1)S(1)}, bf16[384,1152]{1,0:T(8,128)(2,1)}, u32[]{:S(2)}) %copy-start) | copy-done | bytes 884760
  2.5 0.0 copy-start.1
  2.5 1.2 %copy-done.1 = bf16[384,1152]{1,0:T(8,128)(2,1)S(1)} copy-done((bf16[384,1152]{1,0:T(8,128)(2,1)S(1)}, bf16[384,1152]{1,0:T(8,128)(2,1)}, u32[]{:S(2)}) %copy-start.1) | copy-done | bytes 884760
  3.6 0.0 copy-start.3
  3.6 1.0 %copy-done.3 = bf16[2,16,16,384]{3,2,1,0:T(8,128)(2,1)S(1)} copy-done((bf16[2,16,16,384]{3,2,1,0:T(8,128)(2,1)S(1)}, bf16[2,16,16,384]{3,2,1,0:T(8,128)(2,1)}, u32[]{:S(2)}) %copy-start.3) | copy-done | bytes 393240
  4.6 0.0 copy-start.4
  4.6 1.0 %copy-done.4 = bf16[2,16,16,384]{3,2,1,0:T(8,128)(2,1)S(1)} copy-done((bf16[2,16,16,384]{3,2,1,0:T(8,128)(2,1)S(1)}, bf16[2,16,16,384]{3,2,1,0:T(8,128)(2,1)}, u32[]{:S(2)}) %copy-start.4) | copy-done | bytes 393240
  5.6 0.0 copy-start.5
  5.6 1.0 copy-done.5
  6.6 0.0 copy-start.6
  6.6 1.0 copy-done.6
  7.6 0.0 copy-start.8
  7.6 0.7 copy-done.8
  8.3 83.4 %layer.1 = (bf16[2,16,16,384]{3,2,1,0:T(8,128)(2,1)S(1)}, bf16[8,48,128]{2,1,0:T(8,128)(2,1)S(1)}) custom-call(bf16[512,384]{1,0:T(8,128)(2,1)S(1)} %bitcast.4, bf16[512,384]{1,0:T(8,128)(2,1)S(1)} %bitcast.5, s32[32,16]{1,0:T(8,128)S(1)} %bitcast.6, bf16[384,1152]{1,0:T(8,128)(2,1)S(1)} %copy-done, bf16[384,384]{1,0:T(8,128)(2,1)S(1)} %copy-done.5, ...), custom_call_target="tpu_custom_call" | custom-call | tf_op jit(solution)/shard_map/layer/pallas_call | solution.py:478
  91.7 0.0 copy-start.2
  91.7 0.7 copy-done.2
  92.4 0.0 copy-start.7
  92.4 0.6 copy-done.7
  93.0 2.0 %finish.1 = (bf16[512,384]{1,0:T(8,128)(2,1)}, f32[48,18]{1,0:T(8,128)}, f32[48,6]{1,0:T(8,128)}) custom-call(bf16[2,16,16,384]{3,2,1,0:T(8,128)(2,1)} %copy-done.2, bf16[8,48,128]{2,1,0:T(8,128)(2,1)} %copy-done.7), custom_call_target="tpu_custom_call" | custom-call | tf_op jit(solution)/shard_map/finish/pallas_call | solution.py:541
  95.1 0.0 copy-start.11
  95.1 1.4 %copy.13 = f32[48,6]{0,1:T(8,128)} copy(f32[48,6]{1,0:T(8,128)} %get-tuple-element.15) | data formatting | bytes 2304
  96.5 0.0 copy-done.11
  96.5 0.7 copy.12
Async XLA Ops:
  0.6 0.7 copy-start.9
  0.6 0.7 copy-start.10
  1.3 1.2 %copy-start = (bf16[384,1152]{1,0:T(8,128)(2,1)S(1)}, bf16[384,1152]{1,0:T(8,128)(2,1)}, u32[]{:S(2)}) copy-start(bf16[384,1152]{1,0:T(8,128)(2,1)} %time_project_hbm.1) | copy-start | bytes 2654212
  2.5 1.2 %copy-start.1 = (bf16[384,1152]{1,0:T(8,128)(2,1)S(1)}, bf16[384,1152]{1,0:T(8,128)(2,1)}, u32[]{:S(2)}) copy-start(bf16[384,1152]{1,0:T(8,128)(2,1)} %column_project_hbm.1) | copy-start | bytes 2654212
  3.6 1.0 %copy-start.3 = (bf16[2,16,16,384]{3,2,1,0:T(8,128)(2,1)S(1)}, bf16[2,16,16,384]{3,2,1,0:T(8,128)(2,1)}, u32[]{:S(2)}) copy-start(bf16[2,16,16,384]{3,2,1,0:T(8,128)(2,1)} %param.9) | copy-start | bytes 1179652
  4.6 1.0 %copy-start.4 = (bf16[2,16,16,384]{3,2,1,0:T(8,128)(2,1)S(1)}, bf16[2,16,16,384]{3,2,1,0:T(8,128)(2,1)}, u32[]{:S(2)}) copy-start(bf16[2,16,16,384]{3,2,1,0:T(8,128)(2,1)} %param.17) | copy-start | bytes 1179652
  5.6 1.0 copy-start.5
  6.6 1.0 copy-start.6
  7.6 0.7 copy-start.8
  91.7 0.7 copy-start.2
  92.4 0.6 copy-start.7
  95.1 1.4 %copy-start.11 = (f32[48,18]{1,0:T(8,128)S(1)}, f32[48,18]{1,0:T(8,128)}, u32[]{:S(2)}) copy-start(f32[48,18]{1,0:T(8,128)} %get-tuple-element.14) | copy-start | bytes 10372

commit v3 on v2

--- a/solution.py
+++ b/solution.py
@@ -462,8 +462,9 @@
     total = r4[0].astype(f32)
     for index in range(1, 8):
         total = total + r4[index].astype(f32)
-    project_grad_ref[...] = total[:, 0:18]
-    output_grad_ref[...] = total[:, 18:24]
+    turned = jnp.transpose(jnp.concatenate([total, jnp.zeros((80, 128), f32)], axis=0))
+    project_grad_ref[...] = turned[0:18, 0:48]
+    output_grad_ref[...] = turned[18:24, 0:48]
 
 
 VM = pl.BlockSpec(memory_space=pltpu.VMEM)
@@ -535,21 +536,27 @@
         ),
         name="layer",
     )(
-        tokens.reshape(512, D), cotangent.reshape(512, D), clear_flags.reshape(32, 16),
-        time_project, time_output, column_project, column_output, date_numbers, decay_slopes,
+        *(
+            pltpu.with_memory_space_constraint(value, pltpu.HBM)
+            for value in (
+                tokens.reshape(512, D), cotangent.reshape(512, D), clear_flags.reshape(32, 16),
+                time_project, time_output, column_project, column_output, date_numbers, decay_slopes,
+            )
+        )
     )
     mixed, project_grad, output_grad = pl.pallas_call(
         finish_kernel,
         out_shape=(
             jax.ShapeDtypeStruct((512, D), bf16),
-            jax.ShapeDtypeStruct((48, 18), f32),
-            jax.ShapeDtypeStruct((48, 6), f32),
+            jax.ShapeDtypeStruct((18, 48), f32),
+            jax.ShapeDtypeStruct((6, 48), f32),
         ),
         in_specs=[VM] * 2,
         out_specs=(VM, VM, VM),
+        compiler_params=pltpu.CompilerParams(vmem_limit_bytes=8 * 1024 * 1024),
         name="finish",
     )(recv_c, r4)
-    return mixed.reshape(tokens.shape), project_grad, output_grad
+    return mixed.reshape(tokens.shape), project_grad.T, output_grad.T
 
 
 def solution(mesh):

time: 97.7 us -> 84.5 us (0.86)
  local copies, waits for them, and re-layouts: 11.1 us -> 0 us
  Pallas kernels: 85.4 us -> 83.7 us
    unnamed x26 -> x0, local copies, waits for them, and re-layouts: 11.1 us -> none
    pallas_call x1, Pallas kernels: 2.05 us -> 1.04 us  [body(): pl.pallas_call(finish_kernel, out_shape=(jax.ShapeDtypeStruct((512, D), b...]
where the time goes in v3:
time: 84.5 us; the launch traced here: 84.4 us
  Pallas kernels  83.7 us (99%)
    pallas_call x1, Pallas kernels, body(): pl.pallas_call(layer_kernel, out_shape=(jax.ShapeDtypeStruct((2, 16, 16,...  82.7 us

profile of v3, /device:TPU:1, one launch (start us, length us, event | category | flops | bytes accessed | tf_op | source)
XLA Modules:
  0.0 84.4 jit_solution(3135069537029183405)
XLA Ops:
  0.6 82.7 %layer.1 = (bf16[2,16,16,384]{3,2,1,0:T(8,128)(2,1)S(1)}, bf16[8,48,128]{2,1,0:T(8,128)(2,1)S(1)}) custom-call(bf16[512,384]{1,0:T(8,128)(2,1)} %bitcast.6, bf16[512,384]{1,0:T(8,128)(2,1)} %bitcast.7, s32[32,16]{1,0:T(8,128)} %bitcast.8, bf16[384,1152]{1,0:T(8,128)(2,1)} %time_project_hbm.1, bf16[384,384]{1,0:T(8,128)(2,1)} %time_output_hbm.1, ...), custom_call_target="tpu_custom_call" | custom-call | tf_op jit(solution)/shard_map/layer/pallas_call | solution.py:479
  83.3 1.0 %finish.1 = (bf16[512,384]{1,0:T(8,128)(2,1)}, f32[18,48]{1,0:T(8,128)}, f32[6,48]{1,0:T(8,128)}) custom-call(bf16[2,16,16,384]{3,2,1,0:T(8,128)(2,1)S(1)} %get-tuple-element.8.recv_c, bf16[8,48,128]{2,1,0:T(8,128)(2,1)S(1)} %get-tuple-element.9.r4), custom_call_target="tpu_custom_call" | custom-call | tf_op jit(solution)/shard_map/finish/pallas_call | solution.py:547

commit v4 on v3

--- a/solution.py
+++ b/solution.py
@@ -101,7 +101,7 @@
     sa, ra, ss, rs, sc, sb, rb_ref, rc_ref, side, gap_ref, info_ref, base, qkv, heads,
     plane, normed, heads_grad, qkv_grad, send_c, natural, partial_x, partial_y,
     s1, r1, s2x, r2x, s3x, r3x, s2y, r2y, s3y, r3y, s4,
-    sem, grad_sem, load_sem,
+    sem, grad_sem, load_sem, b_sem,
 ):
     d, r = lax.axis_index("date"), lax.axis_index("row")
     parity, octet, kk = d % 2, d // 8, (d // 2) % 4
@@ -203,9 +203,11 @@
         load.wait()
 
     wait_bytes(ra, sem.at[1])
-    source = ((row & 127) >> 1) * 8 + (row & 1) * 4 + (row >> 7)
+    source = (((row >> 1) & 31) * 2 + ((row >> 6) & 1)) * 8 + (row & 1) * 4 + (row >> 7)
     ordered = matmul(one_hot(source, 512), ra[...].reshape(512, D)).astype(bf16)
-    base[...] = ordered
+    for piece in range(8):
+        patch, half = piece // 2, piece % 2
+        base[half, 64 * patch : 64 * patch + 64] = ordered[64 * piece : 64 * piece + 64]
     qkv[...] = matmul(rms_norm(ordered), project_ref[...]).astype(bf16)
 
     wait_bytes(rs, sem.at[3])
@@ -217,7 +219,9 @@
     for when in range(2):
         wanted = jnp.where(pick_row < 4, when * 16 + 4 * kk + pick_row, 32 + when + 2 * (pick_row - 4))
         picked = contract_last(jnp.where(pick_lane == wanted, 1.0, 0.0).astype(bf16), side_low)
-        spread = jnp.where(iota((64, 128), 1) == 2 * iota((64, 128), 0) + when, 1.0, 0.0).astype(bf16)
+        giver = iota((64, 128), 0)
+        place = (giver & 1) * 64 + (giver >> 1) * 2 + when
+        spread = jnp.where(iota((64, 128), 1) == place, 1.0, 0.0).astype(bf16)
         info = info + matmul(picked.astype(bf16), spread)
     info_ref[...] = info
     days = info[4:5] * 32.0 + info[5:6]
@@ -225,41 +229,51 @@
     days_down = jnp.sum(jnp.where(same_date, days, 0.0), axis=1, keepdims=True)
     gap_ref[...] = jnp.abs(days_down - days)
 
-    def time_patch(patch, carry):
-        rows = pl.ds(pl.multiple_of(patch * 128, 128), 128)
+    def time_patch(half, patch):
+        rows = pl.ds(pl.multiple_of(patch * 128 + half * 64, 64), 64)
+        keys_rows = pl.ds(pl.multiple_of(patch * 128, 128), 128)
+        out_rows = pl.ds(pl.multiple_of(patch * 64, 64), 64)
         masks = head_masks()
-        allowed = (info_ref[pl.ds(patch, 1), :] > 0.5) | (iota((128, 128), 0) == iota((128, 128), 1))
+        allowed = (info_ref[pl.ds(patch, 1), :] > 0.5) | (
+            iota((64, 128), 0) + 64 * half == iota((64, 128), 1)
+        )
+        gap = gap_ref[pl.ds(pl.multiple_of(half * 64, 64), 64), :]
         for group in range(GROUPS):
             queries = qkv[rows, 128 * group : 128 * group + 128]
-            keys = stacked(qkv[rows, D + 128 * group : D + 128 * group + 128], masks)
-            values = stacked(qkv[rows, 2 * D + 128 * group : 2 * D + 128 * group + 128], masks)
+            keys = stacked(qkv[keys_rows, D + 128 * group : D + 128 * group + 128], masks)
+            values = stacked(qkv[keys_rows, 2 * D + 128 * group : 2 * D + 128 * group + 128], masks)
             scores = contract_last(queries, keys)
             weights = []
             for head in range(4):
                 block = scores[:, 128 * head : 128 * head + 128] * inverse_root
-                block = block + (-slopes_ref[4 * group + head]) * gap_ref[...]
+                block = block + (-slopes_ref[4 * group + head]) * gap
                 block = jnp.where(allowed, block, masked_score)
                 weights.append(softmax_block(block).astype(bf16))
-            heads[rows, 128 * group : 128 * group + 128] = matmul(
+            heads[out_rows, 128 * group : 128 * group + 128] = matmul(
                 jnp.concatenate(weights, axis=1), values
             ).astype(bf16)
-        return carry
-
-    slot = 2 * (4 * r + kk)
+
+    slot = 4 * r + kk
     home = r == octet
 
     def time_half(half, carry):
-        lax.fori_loop(2 * half, 2 * half + 2, time_patch, 0)
-        rows = pl.ds(pl.multiple_of(half * 256, 256), 256)
-        hidden = (base[rows, :].astype(f32) + matmul(heads[rows, :], output_ref[...])).astype(bf16)
+        def time_pair(pair, inner):
+            time_patch(half, 2 * pair)
+            time_patch(half, 2 * pair + 1)
+            return inner
+
+        lax.fori_loop(0, 2, time_pair, 0)
+        hidden = (
+            base[half].astype(f32) + matmul(heads[0:256, :], output_ref[...])
+        ).astype(bf16)
         small = iota((256, 1), 0)
-        source = ((small >> 2) & 1) * 128 + (small >> 3) * 4 + (small & 3)
+        source = ((small >> 1) & 3) * 64 + (small >> 3) * 2 + (small & 1)
         sb[half] = matmul(one_hot(source, 256), hidden).astype(bf16).reshape(32, 8, D)
 
         def send_hidden(step, inner):
             to = (d // 2 + swing(step, 32)) % 32
             remote(
-                sb.at[half, to], rb_ref.at[slot + half], sem.at[6], sem.at[7],
+                sb.at[half, to], rb_ref.at[half, slot], b_sem.at[half], b_sem.at[2 + half],
                 (2 * to + parity, octet),
             ).start()
             return inner
@@ -268,12 +282,12 @@
 
         @pl.when(home)
         def _():
-            pltpu.make_async_copy(sb.at[half, d // 2], rb_ref.at[slot + half], sem.at[7]).start()
+            pltpu.make_async_copy(sb.at[half, d // 2], rb_ref.at[half, slot], b_sem.at[2 + half]).start()
 
         @pl.when(jnp.logical_not(home))
         def _():
             remote(
-                sb.at[half, d // 2], rb_ref.at[slot + half], sem.at[6], sem.at[7], (d, octet)
+                sb.at[half, d // 2], rb_ref.at[half, slot], b_sem.at[half], b_sem.at[2 + half], (d, octet)
             ).start()
 
         return carry
@@ -282,15 +296,6 @@
 
     wait_bytes(rc_ref, sem.at[5])
     heads_grad[...] = contract_last(rc_ref[...].reshape(512, D), column_output_ref[...]).astype(bf16)
-    wait_bytes(rb_ref, sem.at[7])
-
-    source = ((row & 127) >> 2) * 16 + (row & 3) * 4 + (row >> 7)
-    hidden = matmul(one_hot(source, 512), rb_ref[...].reshape(512, D)).astype(bf16)
-    plane[...] = hidden
-    column_normed = rms_norm(hidden)
-    normed[...] = column_normed
-    qkv[...] = matmul(column_normed, column_project_ref[...]).astype(bf16)
-
     def column_date(date, carry):
         rows = pl.ds(pl.multiple_of(date * 128, 128), 128)
         masks = head_masks()
@@ -346,7 +351,19 @@
 
         return carry
 
-    lax.fori_loop(0, 4, column_date, 0)
+    def column_half(half, carry):
+        wait_bytes(rb_ref.at[half], b_sem.at[2 + half])
+        rows = pl.ds(pl.multiple_of(half * 256, 256), 256)
+        small = iota((256, 1), 0)
+        source = (small & 127) * 2 + (small >> 7)
+        hidden = matmul(one_hot(source, 256), rb_ref[half].reshape(256, D)).astype(bf16)
+        plane[rows, :] = hidden
+        column_normed = rms_norm(hidden)
+        normed[rows, :] = column_normed
+        qkv[rows, :] = matmul(column_normed, column_project_ref[...]).astype(bf16)
+        return lax.fori_loop(2 * half, 2 * half + 2, column_date, carry)
+
+    lax.fori_loop(0, 2, column_half, 0)
 
     natural[0:1152] = contract_rows(qkv_grad[...], normed[...])
     natural[1152:1536] = contract_rows(rc_ref[...].reshape(512, D), heads[...])
@@ -430,12 +447,13 @@
     wait_bytes(sa.at[pl.ds(0, 63)], sem.at[0])
     wait_bytes(rs.at[pl.ds(0, 63)], sem.at[2])
     wait_bytes(sc.at[pl.ds(0, 30)], sem.at[4])
-    wait_bytes(sb.at[0], sem.at[6])
-    wait_bytes(sb.at[1, pl.ds(0, 30)], sem.at[6])
+    for half in range(2):
+        wait_bytes(sb.at[half, pl.ds(0, 31)], b_sem.at[half])
 
     @pl.when(jnp.logical_not(home))
     def _():
-        wait_bytes(sb.at[0, pl.ds(0, 2)], sem.at[6])
+        for half in range(2):
+            wait_bytes(sb.at[half, 0], b_sem.at[half])
 
     wait_bytes(send_c.at[pl.ds(0, 3)], sem.at[8])
     wait_bytes(send_c.at[3, pl.ds(0, 6)], sem.at[8])
@@ -500,12 +518,12 @@
             vmem((64, 1, 128), f32),
             vmem((32, 16, D), bf16),
             vmem((2, 32, 8, D), bf16),
-            vmem((64, 8, D), bf16),
+            vmem((2, 32, 8, D), bf16),
             vmem((4, 128, D), bf16),
             vmem((64, 128), f32),
             vmem((128, 128), f32),
             vmem((8, 128), f32),
-            vmem((512, D), bf16),
+            vmem((2, 256, D), bf16),
             vmem((512, 3 * D), bf16),
             vmem((512, D), bf16),
             vmem((512, D), bf16),
@@ -530,6 +548,7 @@
             pltpu.SemaphoreType.DMA((10,)),
             pltpu.SemaphoreType.DMA((20,)),
             pltpu.SemaphoreType.DMA((9,)),
+            pltpu.SemaphoreType.DMA((4,)),
         ],
         compiler_params=pltpu.CompilerParams(
             collective_id=0, has_side_effects=True, vmem_limit_bytes=48 * 1024 * 1024

time: 84.5 us -> 82.7 us (0.979)
  Pallas kernels: 83.7 us -> 81.9 us
    pallas_call x1, Pallas kernels: 82.7 us -> 80.9 us  [body(): pl.pallas_call(layer_kernel, out_shape=(jax.ShapeDtypeStruct((2, 16, 16,...]
where the time goes in v4:
time: 82.7 us; the launch traced here: 82.6 us
  Pallas kernels  81.9 us (99%)
    pallas_call x1, Pallas kernels, body(): pl.pallas_call(layer_kernel, out_shape=(jax.ShapeDtypeStruct((2, 16, 16,...  80.9 us

profile of v4, /device:TPU:1, one launch (start us, length us, event | category | flops | bytes accessed | tf_op | source)
XLA Modules:
  0.0 82.6 jit_solution(14134240993517286879)
XLA Ops:
  0.6 80.9 %layer.1 = (bf16[2,16,16,384]{3,2,1,0:T(8,128)(2,1)S(1)}, bf16[8,48,128]{2,1,0:T(8,128)(2,1)S(1)}) custom-call(bf16[512,384]{1,0:T(8,128)(2,1)} %bitcast.6, bf16[512,384]{1,0:T(8,128)(2,1)} %bitcast.7, s32[32,16]{1,0:T(8,128)} %bitcast.8, bf16[384,1152]{1,0:T(8,128)(2,1)} %time_project_hbm.1, bf16[384,384]{1,0:T(8,128)(2,1)} %time_output_hbm.1, ...), custom_call_target="tpu_custom_call" | custom-call | tf_op jit(solution)/shard_map/layer/pallas_call | solution.py:497
  81.5 1.0 %finish.1 = (bf16[512,384]{1,0:T(8,128)(2,1)}, f32[18,48]{1,0:T(8,128)}, f32[6,48]{1,0:T(8,128)}) custom-call(bf16[2,16,16,384]{3,2,1,0:T(8,128)(2,1)S(1)} %get-tuple-element.8.recv_c, bf16[8,48,128]{2,1,0:T(8,128)(2,1)S(1)} %get-tuple-element.9.r4), custom_call_target="tpu_custom_call" | custom-call | tf_op jit(solution)/shard_map/finish/pallas_call | solution.py:566

commit v5 on v4

--- a/solution.py
+++ b/solution.py
@@ -88,8 +88,8 @@
 
 
 def swing(step, count):
-    half = (step + 1) // 2
-    return jnp.where(step % 2 == 1, half, count - half)
+    half = lax.div(step + 1, 2)
+    return jnp.where(lax.rem(step, 2) == 1, half, count - half)
 
 
 def layer_kernel(
@@ -122,22 +122,22 @@
         load.start()
 
     def greet_same_row(step, carry):
-        signal(((d + step) % 64, r))
+        signal((lax.rem(d + step, 64), r))
         return carry
 
     def greet_targets(step, carry):
         signal((2 * step + parity, octet))
-        signal((8 * r + 2 * (step // 8) + parity, step % 8))
+        signal((8 * r + 2 * lax.div(step, 8) + parity, lax.rem(step, 8)))
         return carry
 
     def greet_columns(step, carry):
-        to = (own + step) % 16
-        signal((d - parity + to // 8, to % 8))
-        return carry
-
-    lax.fori_loop(1, 64, greet_same_row, 0)
-    lax.fori_loop(0, 32, greet_targets, 0)
-    lax.fori_loop(1, 16, greet_columns, 0)
+        to = lax.rem(own + step, 16)
+        signal((d - parity + lax.div(to, 8), lax.rem(to, 8)))
+        return carry
+
+    lax.fori_loop(1, 64, greet_same_row, 0, unroll=9)
+    lax.fori_loop(0, 32, greet_targets, 0, unroll=8)
+    lax.fori_loop(1, 16, greet_columns, 0, unroll=5)
     signal(partner)
     for index in range(8):
         signal((d - 4 * z_lo + 4 * core, index))
@@ -165,27 +165,27 @@
     pl.semaphore_wait(pltpu.get_barrier_semaphore(), 63 + 64 + 15 + 1 + 16)
 
     def send_tokens(step, carry):
-        to = (d + swing(step, 64)) % 64
+        to = lax.rem(d + swing(step, 64), 64)
         remote(sa.at[to], ra.at[d], sem.at[0], sem.at[1], (to, r)).start()
         return carry
 
     def send_side(step, carry):
-        to = (d + swing(step, 64)) % 64
-        side_of = (to % 2) * 8 + to // 8
+        to = lax.rem(d + swing(step, 64), 64)
+        side_of = lax.rem(to, 2) * 8 + lax.div(to, 8)
         remote(ss.at[side_of], rs.at[d], sem.at[2], sem.at[3], (to, r)).start()
         return carry
 
     def send_cotangent(step, carry):
-        to = (own + step) % 16
+        to = lax.rem(own + step, 16)
         for when in range(2):
             remote(
                 sc.at[2 * to + when],
                 rc_ref.at[2 * parity + when, pl.ds(pl.multiple_of(16 * r, 16), 16)],
-                sem.at[4], sem.at[5], (d - parity + to // 8, to % 8),
+                sem.at[4], sem.at[5], (d - parity + lax.div(to, 8), lax.rem(to, 8)),
             ).start()
         return carry
 
-    lax.fori_loop(1, 64, send_tokens, 0)
+    lax.fori_loop(1, 64, send_tokens, 0, unroll=3)
     pltpu.make_async_copy(sa.at[d], ra.at[d], sem.at[1]).start()
     lax.fori_loop(1, 64, send_side, 0)
     pltpu.make_async_copy(ss.at[parity * 8 + octet], rs.at[d], sem.at[3]).start()
@@ -203,11 +203,11 @@
         load.wait()
 
     wait_bytes(ra, sem.at[1])
-    source = (((row >> 1) & 31) * 2 + ((row >> 6) & 1)) * 8 + (row & 1) * 4 + (row >> 7)
+    source = ((row & 31) * 2 + ((row >> 6) & 1)) * 8 + ((row >> 5) & 1) * 4 + (row >> 7)
     ordered = matmul(one_hot(source, 512), ra[...].reshape(512, D)).astype(bf16)
-    for piece in range(8):
-        patch, half = piece // 2, piece % 2
-        base[half, 64 * patch : 64 * patch + 64] = ordered[64 * piece : 64 * piece + 64]
+    for piece in range(16):
+        patch, part = piece // 4, piece % 4
+        base[part, 32 * patch : 32 * patch + 32] = ordered[32 * piece : 32 * piece + 32]
     qkv[...] = matmul(rms_norm(ordered), project_ref[...]).astype(bf16)
 
     wait_bytes(rs, sem.at[3])
@@ -220,7 +220,7 @@
         wanted = jnp.where(pick_row < 4, when * 16 + 4 * kk + pick_row, 32 + when + 2 * (pick_row - 4))
         picked = contract_last(jnp.where(pick_lane == wanted, 1.0, 0.0).astype(bf16), side_low)
         giver = iota((64, 128), 0)
-        place = (giver & 1) * 64 + (giver >> 1) * 2 + when
+        place = (giver & 1) * 64 + when * 32 + (giver >> 1)
         spread = jnp.where(iota((64, 128), 1) == place, 1.0, 0.0).astype(bf16)
         info = info + matmul(picked.astype(bf16), spread)
     info_ref[...] = info
@@ -230,14 +230,14 @@
     gap_ref[...] = jnp.abs(days_down - days)
 
     def time_patch(half, patch):
-        rows = pl.ds(pl.multiple_of(patch * 128 + half * 64, 64), 64)
+        rows = pl.ds(pl.multiple_of(patch * 128 + half * 32, 32), 32)
         keys_rows = pl.ds(pl.multiple_of(patch * 128, 128), 128)
-        out_rows = pl.ds(pl.multiple_of(patch * 64, 64), 64)
+        out_rows = pl.ds(pl.multiple_of(patch * 32, 32), 32)
         masks = head_masks()
         allowed = (info_ref[pl.ds(patch, 1), :] > 0.5) | (
-            iota((64, 128), 0) + 64 * half == iota((64, 128), 1)
+            iota((32, 128), 0) + 32 * half == iota((32, 128), 1)
         )
-        gap = gap_ref[pl.ds(pl.multiple_of(half * 64, 64), 64), :]
+        gap = gap_ref[pl.ds(pl.multiple_of(half * 32, 32), 32), :]
         for group in range(GROUPS):
             queries = qkv[rows, 128 * group : 128 * group + 128]
             keys = stacked(qkv[keys_rows, D + 128 * group : D + 128 * group + 128], masks)
@@ -264,16 +264,16 @@
 
         lax.fori_loop(0, 2, time_pair, 0)
         hidden = (
-            base[half].astype(f32) + matmul(heads[0:256, :], output_ref[...])
+            base[half].astype(f32) + matmul(heads[0:128, :], output_ref[...])
         ).astype(bf16)
-        small = iota((256, 1), 0)
-        source = ((small >> 1) & 3) * 64 + (small >> 3) * 2 + (small & 1)
-        sb[half] = matmul(one_hot(source, 256), hidden).astype(bf16).reshape(32, 8, D)
+        small = iota((128, 1), 0)
+        source = (small & 3) * 32 + (small >> 2)
+        sb[half] = matmul(one_hot(source, 128), hidden).reshape(32, 4, D).astype(bf16)
 
         def send_hidden(step, inner):
-            to = (d // 2 + swing(step, 32)) % 32
+            to = lax.rem(lax.div(d, 2) + swing(step, 32), 32)
             remote(
-                sb.at[half, to], rb_ref.at[half, slot], b_sem.at[half], b_sem.at[2 + half],
+                sb.at[half, to], rb_ref.at[half, slot], b_sem.at[half], b_sem.at[4 + half],
                 (2 * to + parity, octet),
             ).start()
             return inner
@@ -282,17 +282,17 @@
 
         @pl.when(home)
         def _():
-            pltpu.make_async_copy(sb.at[half, d // 2], rb_ref.at[half, slot], b_sem.at[2 + half]).start()
+            pltpu.make_async_copy(sb.at[half, d // 2], rb_ref.at[half, slot], b_sem.at[4 + half]).start()
 
         @pl.when(jnp.logical_not(home))
         def _():
             remote(
-                sb.at[half, d // 2], rb_ref.at[half, slot], b_sem.at[half], b_sem.at[2 + half], (d, octet)
+                sb.at[half, d // 2], rb_ref.at[half, slot], b_sem.at[half], b_sem.at[4 + half], (d, octet)
             ).start()
 
         return carry
 
-    lax.fori_loop(0, 2, time_half, 0)
+    lax.fori_loop(0, 4, time_half, 0)
 
     wait_bytes(rc_ref, sem.at[5])
     heads_grad[...] = contract_last(rc_ref[...].reshape(512, D), column_output_ref[...]).astype(bf16)
@@ -326,12 +326,16 @@
             qkv_grad[rows, 2 * D + 128 * group : 2 * D + 128 * group + 128] = unstacked(
                 contract_rows(low, outer), masks
             ).astype(bf16)
+        return carry
+
+    def send_mixed(date, carry):
+        rows = pl.ds(pl.multiple_of(date * 128, 128), 128)
         mixed = plane[rows, :].astype(f32) + matmul(heads[rows, :], column_output_ref[...])
         send_c[date] = mixed.astype(bf16).reshape(8, 16, D)
         to_date = d - parity + date // 2
 
         def send_rows(step, inner):
-            to = (r + swing(step, 8)) % 8
+            to = lax.rem(r + swing(step, 8), 8)
             remote(
                 send_c.at[date, to], recv_c.at[date % 2, own], sem.at[8], sem.at[9], (to_date, to)
             ).start()
@@ -352,18 +356,22 @@
         return carry
 
     def column_half(half, carry):
-        wait_bytes(rb_ref.at[half], b_sem.at[2 + half])
-        rows = pl.ds(pl.multiple_of(half * 256, 256), 256)
-        small = iota((256, 1), 0)
-        source = (small & 127) * 2 + (small >> 7)
-        hidden = matmul(one_hot(source, 256), rb_ref[half].reshape(256, D)).astype(bf16)
+        wait_bytes(rb_ref.at[half], b_sem.at[4 + half])
+        rows = pl.ds(pl.multiple_of(half * 128, 128), 128)
+        hidden = rb_ref[half].reshape(128, D)
         plane[rows, :] = hidden
         column_normed = rms_norm(hidden)
         normed[rows, :] = column_normed
         qkv[rows, :] = matmul(column_normed, column_project_ref[...]).astype(bf16)
-        return lax.fori_loop(2 * half, 2 * half + 2, column_date, carry)
-
-    lax.fori_loop(0, 2, column_half, 0)
+        column_date(half, 0)
+
+        @pl.when(half < 2)
+        def _():
+            send_mixed(half, 0)
+
+        return carry
+
+    lax.fori_loop(0, 4, column_half, 0)
 
     natural[0:1152] = contract_rows(qkv_grad[...], normed[...])
     natural[1152:1536] = contract_rows(rc_ref[...].reshape(512, D), heads[...])
@@ -410,6 +418,7 @@
         size = first_axis[1]
         sent[...] = (mine + r1[chunk].astype(f32)).astype(bf16).reshape(size, 768 // size, 128)
         exchange(first_axis, sent, received, grad_sem.at[6 + chunk], grad_sem.at[9 + chunk])
+    lax.fori_loop(2, 4, send_mixed, 0)
     for chunk, _, _, first_axis, sent, received, second_axis, sent_next, received_next in plans:
         total = gathered(first_axis, sent, received, grad_sem.at[9 + chunk])
         sent_next[...] = total.reshape(second_axis[1], 24, 128).astype(bf16)
@@ -447,12 +456,12 @@
     wait_bytes(sa.at[pl.ds(0, 63)], sem.at[0])
     wait_bytes(rs.at[pl.ds(0, 63)], sem.at[2])
     wait_bytes(sc.at[pl.ds(0, 30)], sem.at[4])
-    for half in range(2):
+    for half in range(4):
         wait_bytes(sb.at[half, pl.ds(0, 31)], b_sem.at[half])
 
     @pl.when(jnp.logical_not(home))
     def _():
-        for half in range(2):
+        for half in range(4):
             wait_bytes(sb.at[half, 0], b_sem.at[half])
 
     wait_bytes(send_c.at[pl.ds(0, 3)], sem.at[8])
@@ -517,13 +526,13 @@
             vmem((16, 1, 128), f32),
             vmem((64, 1, 128), f32),
             vmem((32, 16, D), bf16),
-            vmem((2, 32, 8, D), bf16),
-            vmem((2, 32, 8, D), bf16),
+            vmem((4, 32, 4, D), bf16),
+            vmem((4, 32, 4, D), bf16),
             vmem((4, 128, D), bf16),
             vmem((64, 128), f32),
             vmem((128, 128), f32),
             vmem((8, 128), f32),
-            vmem((2, 256, D), bf16),
+            vmem((4, 128, D), bf16),
             vmem((512, 3 * D), bf16),
             vmem((512, D), bf16),
             vmem((512, D), bf16),
@@ -548,7 +557,7 @@
             pltpu.SemaphoreType.DMA((10,)),
             pltpu.SemaphoreType.DMA((20,)),
             pltpu.SemaphoreType.DMA((9,)),
-            pltpu.SemaphoreType.DMA((4,)),
+            pltpu.SemaphoreType.DMA((8,)),
         ],
         compiler_params=pltpu.CompilerParams(
             collective_id=0, has_side_effects=True, vmem_limit_bytes=48 * 1024 * 1024

time: 82.7 us -> 88 us (1.064)
  Pallas kernels: 81.9 us -> 87.2 us
    pallas_call x1, Pallas kernels: 80.9 us -> 86.2 us  [body(): pl.pallas_call(layer_kernel, out_shape=(jax.ShapeDtypeStruct((2, 16, 16,...]
where the time goes in v5:
time: 88 us; the launch traced here: 87.9 us
  Pallas kernels  87.2 us (99%)
    pallas_call x1, Pallas kernels, body(): pl.pallas_call(layer_kernel, out_shape=(jax.ShapeDtypeStruct((2, 16, 16,...  86.2 us

profile of v5, /device:TPU:1, one launch (start us, length us, event | category | flops | bytes accessed | tf_op | source)
XLA Modules:
  0.0 87.9 jit_solution(5594519206104311089)
XLA Ops:
  0.6 86.2 %layer.1 = (bf16[2,16,16,384]{3,2,1,0:T(8,128)(2,1)S(1)}, bf16[8,48,128]{2,1,0:T(8,128)(2,1)S(1)}) custom-call(bf16[512,384]{1,0:T(8,128)(2,1)} %bitcast.6, bf16[512,384]{1,0:T(8,128)(2,1)} %bitcast.7, s32[32,16]{1,0:T(8,128)} %bitcast.8, bf16[384,1152]{1,0:T(8,128)(2,1)} %time_project_hbm.1, bf16[384,384]{1,0:T(8,128)(2,1)} %time_output_hbm.1, ...), custom_call_target="tpu_custom_call" | custom-call | tf_op jit(solution)/shard_map/layer/pallas_call | solution.py:506
  86.8 1.0 %finish.1 = (bf16[512,384]{1,0:T(8,128)(2,1)}, f32[18,48]{1,0:T(8,128)}, f32[6,48]{1,0:T(8,128)}) custom-call(bf16[2,16,16,384]{3,2,1,0:T(8,128)(2,1)S(1)} %get-tuple-element.8.recv_c, bf16[8,48,128]{2,1,0:T(8,128)(2,1)S(1)} %get-tuple-element.9.r4), custom_call_target="tpu_custom_call" | custom-call | tf_op jit(solution)/shard_map/finish/pallas_call | solution.py:575

commit v6 on v4

--- a/solution.py
+++ b/solution.py
@@ -61,8 +61,8 @@
     return total
 
 
-def softmax_block(scores):
-    raised = jnp.exp(scores - jnp.max(scores, axis=-1, keepdims=True))
+def softmax_block(scores, scale=1.0):
+    raised = jnp.exp2((scores - jnp.max(scores, axis=-1, keepdims=True)) * (scale * math.log2(math.e)))
     return raised * (1.0 / jnp.sum(raised, axis=-1, keepdims=True))
 
 
@@ -88,8 +88,8 @@
 
 
 def swing(step, count):
-    half = (step + 1) // 2
-    return jnp.where(step % 2 == 1, half, count - half)
+    half = lax.div(step + 1, 2)
+    return jnp.where(lax.rem(step, 2) == 1, half, count - half)
 
 
 def layer_kernel(
@@ -122,22 +122,22 @@
         load.start()
 
     def greet_same_row(step, carry):
-        signal(((d + step) % 64, r))
+        signal((lax.rem(d + step, 64), r))
         return carry
 
     def greet_targets(step, carry):
         signal((2 * step + parity, octet))
-        signal((8 * r + 2 * (step // 8) + parity, step % 8))
+        signal((8 * r + 2 * lax.div(step, 8) + parity, lax.rem(step, 8)))
         return carry
 
     def greet_columns(step, carry):
-        to = (own + step) % 16
-        signal((d - parity + to // 8, to % 8))
-        return carry
-
-    lax.fori_loop(1, 64, greet_same_row, 0)
-    lax.fori_loop(0, 32, greet_targets, 0)
-    lax.fori_loop(1, 16, greet_columns, 0)
+        to = lax.rem(own + step, 16)
+        signal((d - parity + lax.div(to, 8), lax.rem(to, 8)))
+        return carry
+
+    lax.fori_loop(1, 64, greet_same_row, 0, unroll=9)
+    lax.fori_loop(0, 32, greet_targets, 0, unroll=8)
+    lax.fori_loop(1, 16, greet_columns, 0, unroll=5)
     signal(partner)
     for index in range(8):
         signal((d - 4 * z_lo + 4 * core, index))
@@ -165,27 +165,27 @@
     pl.semaphore_wait(pltpu.get_barrier_semaphore(), 63 + 64 + 15 + 1 + 16)
 
     def send_tokens(step, carry):
-        to = (d + swing(step, 64)) % 64
+        to = lax.rem(d + swing(step, 64), 64)
         remote(sa.at[to], ra.at[d], sem.at[0], sem.at[1], (to, r)).start()
         return carry
 
     def send_side(step, carry):
-        to = (d + swing(step, 64)) % 64
-        side_of = (to % 2) * 8 + to // 8
+        to = lax.rem(d + swing(step, 64), 64)
+        side_of = lax.rem(to, 2) * 8 + lax.div(to, 8)
         remote(ss.at[side_of], rs.at[d], sem.at[2], sem.at[3], (to, r)).start()
         return carry
 
     def send_cotangent(step, carry):
-        to = (own + step) % 16
+        to = lax.rem(own + step, 16)
         for when in range(2):
             remote(
                 sc.at[2 * to + when],
                 rc_ref.at[2 * parity + when, pl.ds(pl.multiple_of(16 * r, 16), 16)],
-                sem.at[4], sem.at[5], (d - parity + to // 8, to % 8),
+                sem.at[4], sem.at[5], (d - parity + lax.div(to, 8), lax.rem(to, 8)),
             ).start()
         return carry
 
-    lax.fori_loop(1, 64, send_tokens, 0)
+    lax.fori_loop(1, 64, send_tokens, 0, unroll=3)
     pltpu.make_async_copy(sa.at[d], ra.at[d], sem.at[1]).start()
     lax.fori_loop(1, 64, send_side, 0)
     pltpu.make_async_copy(ss.at[parity * 8 + octet], rs.at[d], sem.at[3]).start()
@@ -271,7 +271,7 @@
         sb[half] = matmul(one_hot(source, 256), hidden).astype(bf16).reshape(32, 8, D)
 
         def send_hidden(step, inner):
-            to = (d // 2 + swing(step, 32)) % 32
+            to = lax.rem(lax.div(d, 2) + swing(step, 32), 32)
             remote(
                 sb.at[half, to], rb_ref.at[half, slot], b_sem.at[half], b_sem.at[2 + half],
                 (2 * to + parity, octet),
@@ -309,7 +309,7 @@
             products = contract_last(outer, values)
             weights_low, scores_low = [], []
             for head in range(4):
-                weights = softmax_block(scores[:, 128 * head : 128 * head + 128] * inverse_root)
+                weights = softmax_block(scores[:, 128 * head : 128 * head + 128], inverse_root)
                 product = products[:, 128 * head : 128 * head + 128]
                 centre = jnp.sum(weights * product, axis=-1, keepdims=True)
                 weights_low.append(weights.astype(bf16))
@@ -326,12 +326,16 @@
             qkv_grad[rows, 2 * D + 128 * group : 2 * D + 128 * group + 128] = unstacked(
                 contract_rows(low, outer), masks
             ).astype(bf16)
+        return carry
+
+    def send_mixed(date, carry):
+        rows = pl.ds(pl.multiple_of(date * 128, 128), 128)
         mixed = plane[rows, :].astype(f32) + matmul(heads[rows, :], column_output_ref[...])
         send_c[date] = mixed.astype(bf16).reshape(8, 16, D)
         to_date = d - parity + date // 2
 
         def send_rows(step, inner):
-            to = (r + swing(step, 8)) % 8
+            to = lax.rem(r + swing(step, 8), 8)
             remote(
                 send_c.at[date, to], recv_c.at[date % 2, own], sem.at[8], sem.at[9], (to_date, to)
             ).start()
@@ -361,7 +365,13 @@
         column_normed = rms_norm(hidden)
         normed[rows, :] = column_normed
         qkv[rows, :] = matmul(column_normed, column_project_ref[...]).astype(bf16)
-        return lax.fori_loop(2 * half, 2 * half + 2, column_date, carry)
+        lax.fori_loop(2 * half, 2 * half + 2, column_date, 0)
+
+        @pl.when(half == 0)
+        def _():
+            lax.fori_loop(0, 2, send_mixed, 0)
+
+        return carry
 
     lax.fori_loop(0, 2, column_half, 0)
 
@@ -410,6 +420,7 @@
         size = first_axis[1]
         sent[...] = (mine + r1[chunk].astype(f32)).astype(bf16).reshape(size, 768 // size, 128)
         exchange(first_axis, sent, received, grad_sem.at[6 + chunk], grad_sem.at[9 + chunk])
+    lax.fori_loop(2, 4, send_mixed, 0)
     for chunk, _, _, first_axis, sent, received, second_axis, sent_next, received_next in plans:
         total = gathered(first_axis, sent, received, grad_sem.at[9 + chunk])
         sent_next[...] = total.reshape(second_axis[1], 24, 128).astype(bf16)

time: 82.7 us -> 81.4 us (0.984)
  Pallas kernels: 81.9 us -> 80.6 us
    pallas_call x1, Pallas kernels: 80.9 us -> 79.6 us  [body(): pl.pallas_call(layer_kernel, out_shape=(jax.ShapeDtypeStruct((2, 16, 16,...]
where the time goes in v6:
time: 81.4 us; the launch traced here: 81.2 us
  Pallas kernels  80.6 us (99%)
    pallas_call x1, Pallas kernels, body(): pl.pallas_call(layer_kernel, out_shape=(jax.ShapeDtypeStruct((2, 16, 16,...  79.6 us

profile of v6, /device:TPU:1, one launch (start us, length us, event | category | flops | bytes accessed | tf_op | source)
XLA Modules:
  0.0 81.2 jit_solution(16474640561952817550)
XLA Ops:
  0.6 79.6 %layer.1 = (bf16[2,16,16,384]{3,2,1,0:T(8,128)(2,1)S(1)}, bf16[8,48,128]{2,1,0:T(8,128)(2,1)S(1)}) custom-call(bf16[512,384]{1,0:T(8,128)(2,1)} %bitcast.6, bf16[512,384]{1,0:T(8,128)(2,1)} %bitcast.7, s32[32,16]{1,0:T(8,128)} %bitcast.8, bf16[384,1152]{1,0:T(8,128)(2,1)} %time_project_hbm.1, bf16[384,384]{1,0:T(8,128)(2,1)} %time_output_hbm.1, ...), custom_call_target="tpu_custom_call" | custom-call | tf_op jit(solution)/shard_map/layer/pallas_call | solution.py:508
  80.2 1.0 %finish.1 = (bf16[512,384]{1,0:T(8,128)(2,1)}, f32[18,48]{1,0:T(8,128)}, f32[6,48]{1,0:T(8,128)}) custom-call(bf16[2,16,16,384]{3,2,1,0:T(8,128)(2,1)S(1)} %get-tuple-element.8.recv_c, bf16[8,48,128]{2,1,0:T(8,128)(2,1)S(1)} %get-tuple-element.9.r4), custom_call_target="tpu_custom_call" | custom-call | tf_op jit(solution)/shard_map/finish/pallas_call | solution.py:577

commit v7 on v6

--- a/solution.py
+++ b/solution.py
@@ -175,15 +175,22 @@
         remote(ss.at[side_of], rs.at[d], sem.at[2], sem.at[3], (to, r)).start()
         return carry
 
-    def send_cotangent(step, carry):
-        to = lax.rem(own + step, 16)
-        for when in range(2):
+    def send_cotangent(when):
+        def send_one(step, carry):
+            to = lax.rem(own + step, 16)
             remote(
                 sc.at[2 * to + when],
                 rc_ref.at[2 * parity + when, pl.ds(pl.multiple_of(16 * r, 16), 16)],
                 sem.at[4], sem.at[5], (d - parity + lax.div(to, 8), lax.rem(to, 8)),
             ).start()
-        return carry
+            return carry
+
+        lax.fori_loop(1, 16, send_one, 0)
+        pltpu.make_async_copy(
+            sc.at[2 * own + when],
+            rc_ref.at[2 * parity + when, pl.ds(pl.multiple_of(16 * r, 16), 16)],
+            sem.at[5],
+        ).start()
 
     lax.fori_loop(1, 64, send_tokens, 0, unroll=3)
     pltpu.make_async_copy(sa.at[d], ra.at[d], sem.at[1]).start()
@@ -192,17 +199,12 @@
     loads[3].wait()
     source = ((row >> 4) & 1) * 256 + (row & 15) * 16 + (row >> 5)
     sc[...] = matmul(one_hot(source, 512), rc_in[...]).astype(bf16).reshape(32, 16, D)
-    lax.fori_loop(1, 16, send_cotangent, 0)
-    for when in range(2):
-        pltpu.make_async_copy(
-            sc.at[2 * own + when],
-            rc_ref.at[2 * parity + when, pl.ds(pl.multiple_of(16 * r, 16), 16)],
-            sem.at[5],
-        ).start()
+    send_cotangent(0)
     for load in loads[4:]:
         load.wait()
 
     wait_bytes(ra, sem.at[1])
+    send_cotangent(1)
     source = (((row >> 1) & 31) * 2 + ((row >> 6) & 1)) * 8 + (row & 1) * 4 + (row >> 7)
     ordered = matmul(one_hot(source, 512), ra[...].reshape(512, D)).astype(bf16)
     for piece in range(8):

time: 81.4 us -> 81.5 us (level)
  no operation moved by 1% of the time
where the time goes in v7:
time: 81.5 us; the launch traced here: 81.4 us
  Pallas kernels  80.7 us (99%)
    pallas_call x1, Pallas kernels, body(): pl.pallas_call(layer_kernel, out_shape=(jax.ShapeDtypeStruct((2, 16, 16,...  79.7 us

profile of v7, /device:TPU:1, one launch (start us, length us, event | category | flops | bytes accessed | tf_op | source)
XLA Modules:
  0.0 81.4 jit_solution(12499878341604643302)
XLA Ops:
  0.6 79.7 %layer.1 = (bf16[2,16,16,384]{3,2,1,0:T(8,128)(2,1)S(1)}, bf16[8,48,128]{2,1,0:T(8,128)(2,1)S(1)}) custom-call(bf16[512,384]{1,0:T(8,128)(2,1)} %bitcast.6, bf16[512,384]{1,0:T(8,128)(2,1)} %bitcast.7, s32[32,16]{1,0:T(8,128)} %bitcast.8, bf16[384,1152]{1,0:T(8,128)(2,1)} %time_project_hbm.1, bf16[384,384]{1,0:T(8,128)(2,1)} %time_output_hbm.1, ...), custom_call_target="tpu_custom_call" | custom-call | tf_op jit(solution)/shard_map/layer/pallas_call | solution.py:510
  80.3 1.0 %finish.1 = (bf16[512,384]{1,0:T(8,128)(2,1)}, f32[18,48]{1,0:T(8,128)}, f32[6,48]{1,0:T(8,128)}) custom-call(bf16[2,16,16,384]{3,2,1,0:T(8,128)(2,1)S(1)} %get-tuple-element.8.recv_c, bf16[8,48,128]{2,1,0:T(8,128)(2,1)S(1)} %get-tuple-element.9.r4), custom_call_target="tpu_custom_call" | custom-call | tf_op jit(solution)/shard_map/finish/pallas_call | solution.py:579
